TPU v7x, 256 devices: a whole 4x4x8 slice. The times are simulated.
256 devices in a mesh: node: 16 (over x_lo, z), shard: 16 (over x_hi, y, core).
Axes of the slice: x: 4 (x_hi: 2, x_lo: 2; x = x_hi * 2 + x_lo), y: 4, z: 8, core: 2. Of those that a mesh axis runs over, the one named last changes fastest.
Arguments:
- hidden: bfloat16 [16, 2048, 7168], P('node', 'shard'), may hold values from -6 to 6
- cotangent: bfloat16 [16, 2048, 2048], P('node', 'shard'), may hold values from -0.125 to 0.125
- weights: bfloat16 [16, 7168, 2048], P('node', 'shard'), may hold values from -0.59765625 to 0.59765625
- momentum: bfloat16 [16, 7168, 2048], P('node', 'shard'), may hold values from -6 to 6
Outputs:
- new_weights: bfloat16 [16, 7168, 2048], P('node', 'shard')
- new_momentum: bfloat16 [16, 7168, 2048], P('node', 'shard')
All inputs are finite; a program needn't handle non-finite values.
Results may differ from a plain program's by a relative error of at most 0.0085.
Values may be sent and summed in bfloat16 or wider, within the bound.
No kernel may reach another device: no remote copies, remote signals or barrier semaphores. Data moves between devices by JAX's collectives and lax.ppermute only.
A program may use at most 64 MiB of HBM per device.

v0:
```python
import jax
import jax.numpy as jnp
from jax import lax
from jax.sharding import PartitionSpec as P

step_size = 0.1
friction = 0.9


def from_partner(value, axis, distance):
    mask = 2**distance
    pairs = [(source, source ^ mask) for source in range(lax.axis_size(axis))]
    return lax.ppermute(value, axis, pairs)


def on_device(hidden, cotangent, weights, momentum):
    token_acts = hidden[0]
    out_grads = cotangent[0]
    weight_rows = weights[0]
    moment_rows = momentum[0]
    local_cols = lax.all_to_all(token_acts, "shard", split_axis=1, concat_axis=0, tiled=True)
    gradient = lax.dot_general(
        local_cols,
        lax.all_gather(out_grads, "shard", axis=0, tiled=True),
        (((0,), (0,)), ((), ())),
        preferred_element_type=jnp.float32,
    )
    new_moment = (friction * moment_rows.astype(jnp.float32) + gradient).astype(jnp.bfloat16)
    half_step = (
        weight_rows.astype(jnp.float32) - step_size * new_moment.astype(jnp.float32)
    ).astype(jnp.bfloat16)
    west_side = from_partner(half_step, "node", 0)
    east_side = from_partner(west_side, "node", 1)
    north_rows = from_partner(half_step, "node", 2)
    south_rows = from_partner(north_rows, "node", 3)
    candidates = [
        half_step.astype(jnp.float32),
        west_side.astype(jnp.float32),
        east_side.astype(jnp.float32),
        north_rows.astype(jnp.float32),
        south_rows.astype(jnp.float32),
    ]
    running = candidates[0]
    largest = candidates[0]
    smallest = candidates[0]
    for value in candidates[1:]:
        running = running + value
        largest = jnp.maximum(largest, value)
        smallest = jnp.minimum(smallest, value)
    new_weights = ((running - largest - smallest) / 3.0).astype(jnp.bfloat16)
    return (new_weights[None], new_moment[None])


def solution(mesh):
    placed = (
        P("node", "shard", None),
        P("node", "shard", None),
        P("node", "shard", None),
        P("node", "shard", None),
    )
    return jax.shard_map(
        on_device,
        mesh=mesh,
        in_specs=placed,
        out_specs=(P("node", "shard", None), P("node", "shard", None)),
        check_vma=False,
    )
```

profile of v0, /device:TPU:1, one launch (start us, length us, event | category | flops | bytes accessed | tf_op | source)
XLA Modules:
  0.0 328.2 jit_solution(3365000726305444762)
XLA Ops:
  7.2 0.0 all-gather.3.cloned.1.call-start
  7.2 0.7 all-gather.3.cloned.1.call-update
  7.9 3.3 %copy.6 = bf16[1,128,7168]{1,2,0:T(8,128)(2,1)S(1)} copy(bf16[1,128,7168]{2,1,0:T(8,128)(2,1)} %param.4) | data formatting | bytes 3670016 | tf_op args[0]
  11.2 39.6 %all_to_all.19 = bf16[128,16,448]{0,2,1:T(8,128)(2,1)} all-to-all(bf16[128,16,448]{0,2,1:T(8,128)(2,1)S(1)} %bitcast.28), channel_id=1, replica_groups=mesh['node'=16,'shard'=16] {'shard'}, dimensions={1} | all-to-all | bytes 3670016 | tf_op jit(solution)/shard_map/all_to_all | solution.py:21
  50.8 50.8 %all-gather.3.cloned.1.call-done = bf16[1,2048,2048]{2,1,0:T(8,128)(2,1)} async-done(((bf16[1,128,2048]{2,1,0:T(8,128)(2,1)}), bf16[1,2048,2048]{2,1,0:T(8,128)(2,1)}) %all-gather.3.cloned.1.call-update) | async-done | bytes 8388624 | tf_op jit(solution)/shard_map/all_gather | solution.py:24
  101.6 10.4 %fusion.6 = (bf16[448,2048]{1,0:T(8,128)(2,1)S(1)}, bf16[448,2048]{1,0:T(8,128)(2,1)}) fusion(bf16[1,448,2048]{2,1,0:T(8,128)(2,1)} %param.6, bf16[1,2048,2048]{2,1,0:T(8,128)(2,1)} %all-gather.3.cloned.1.call-done, bf16[1,448,2048]{2,1,0:T(8,128)(2,1)} %param.7, bf16[128,16,448]{0,2,1:T(8,128)(2,1)} %all_to_all.19), kind=kOutput, calls=%fused_computation.19 | convolution fusion | flops 3766353920 | bytes 17563648 | tf_op jit(solution)/shard_map/dot_general | solution.py:22
  112.0 5.5 %collective-permute-start.2 = (bf16[448,2048]{1,0:T(8,128)(2,1)S(1)}, bf16[448,2048]{1,0:T(8,128)(2,1)S(1)}, u32[]{:S(2)}, u32[]{:S(2)}) collective-permute-start(bf16[448,2048]{1,0:T(8,128)(2,1)S(1)} %get-tuple-element.2), channel_id=1, source_target_pairs={{0,64},{16,80},{32,96},{48,112},{64,0},{80,16},{96,32},{112,48},{1... | collective-permute-start | bytes 5505032 | tf_op jit(solution)/shard_map/ppermute | solution.py:13
  117.5 0.4 collective-permute-start
  117.9 67.1 %collective-permute-done.2 = bf16[448,2048]{1,0:T(8,128)(2,1)S(1)} collective-permute-done((bf16[448,2048]{1,0:T(8,128)(2,1)S(1)}, bf16[448,2048]{1,0:T(8,128)(2,1)S(1)}, u32[]{:S(2)}, u32[]{:S(2)}) %collective-permute-start.2) | collective-permute-done | bytes 1835040 | tf_op jit(solution)/shard_map/ppermute | solution.py:13
  184.9 0.3 collective-permute-start.3
  185.2 51.6 %collective-permute-done = bf16[448,2048]{1,0:T(8,128)(2,1)S(1)} collective-permute-done((bf16[448,2048]{1,0:T(8,128)(2,1)S(1)}, bf16[448,2048]{1,0:T(8,128)(2,1)S(1)}, u32[]{:S(2)}, u32[]{:S(2)}) %collective-permute-start) | collective-permute-done | bytes 1835040 | tf_op jit(solution)/shard_map/ppermute | solution.py:13
  236.8 0.3 collective-permute-start.1
  237.1 0.0 collective-permute-done.3
  237.1 80.8 %collective-permute-done.1 = bf16[448,2048]{1,0:T(8,128)(2,1)S(1)} collective-permute-done((bf16[448,2048]{1,0:T(8,128)(2,1)S(1)}, bf16[448,2048]{1,0:T(8,128)(2,1)S(1)}, u32[]{:S(2)}, u32[]{:S(2)}) %collective-permute-start.1) | collective-permute-done | bytes 1835040 | tf_op jit(solution)/shard_map/ppermute | solution.py:13
  317.9 3.4 %fusion.12 = bf16[1,448,2048]{2,1,0:T(8,128)(2,1)} fusion(bf16[448,2048]{1,0:T(8,128)(2,1)S(1)} %collective-permute-done.3, bf16[448,2048]{1,0:T(8,128)(2,1)S(1)} %collective-permute-done.2, bf16[448,2048]{1,0:T(8,128)(2,1)S(1)} %collective-permute-done.1, bf16[448,2048]{1,0:T(8,128)(2,1)S(1)} %collective-permute-done, bf16[448,2048]{1,0:T(8,128)(2,1)S(1)} %get-tuple-element.2), kind=kLoop, calls=%fused_computation.24 | loop fusion | flops 19267584 | bytes 11010048 | tf_op jit(solution)/shard_map/broadcast_in_dim | solution.py:51
Async XLA Ops:
  7.2 94.5 %all-gather.3.cloned.1.call-start = ((), (), s32[]{:S(2)}) async-start(), calls=%async_computation.1 | async-start | bytes 8912896 | tf_op jit(solution)/shard_map/all_gather | solution.py:24
  112.0 72.9 %collective-permute-start.2 = (bf16[448,2048]{1,0:T(8,128)(2,1)S(1)}, bf16[448,2048]{1,0:T(8,128)(2,1)S(1)}, u32[]{:S(2)}, u32[]{:S(2)}) collective-permute-start(bf16[448,2048]{1,0:T(8,128)(2,1)S(1)} %get-tuple-element.2), channel_id=1, source_target_pairs={{0,64},{16,80},{32,96},{48,112},{64,0},{80,16},{96,32},{112,48},{1... | collective-permute-start | bytes 5505032 | tf_op jit(solution)/shard_map/ppermute | solution.py:13
  117.5 119.3 %collective-permute-start = (bf16[448,2048]{1,0:T(8,128)(2,1)S(1)}, bf16[448,2048]{1,0:T(8,128)(2,1)S(1)}, u32[]{:S(2)}, u32[]{:S(2)}) collective-permute-start(bf16[448,2048]{1,0:T(8,128)(2,1)S(1)} %get-tuple-element.2), channel_id=1, source_target_pairs={{0,16},{16,0},{32,48},{48,32},{64,80},{80,64},{96,112},{112,96},{1... | collective-permute-start | bytes 5505032 | tf_op jit(solution)/shard_map/ppermute | solution.py:13
  184.9 52.2 %collective-permute-start.3 = (bf16[448,2048]{1,0:T(8,128)(2,1)S(1)}, bf16[448,2048]{1,0:T(8,128)(2,1)S(1)}, u32[]{:S(2)}, u32[]{:S(2)}) collective-permute-start(bf16[448,2048]{1,0:T(8,128)(2,1)S(1)} %collective-permute-done.2), channel_id=1, source_target_pairs={{0,128},{16,144},{32,160},{48,176},{64,192},{80,208},{96,224},{112... | collective-permute-start | bytes 5505032 | tf_op jit(solution)/shard_map/ppermute | solution.py:13
  236.8 81.1 %collective-permute-start.1 = (bf16[448,2048]{1,0:T(8,128)(2,1)S(1)}, bf16[448,2048]{1,0:T(8,128)(2,1)S(1)}, u32[]{:S(2)}, u32[]{:S(2)}) collective-permute-start(bf16[448,2048]{1,0:T(8,128)(2,1)S(1)} %collective-permute-done), channel_id=1, source_target_pairs={{0,32},{16,48},{32,0},{48,16},{64,96},{80,112},{96,64},{112,80},{1... | collective-permute-start | bytes 5505032 | tf_op jit(solution)/shard_map/ppermute | solution.py:13
Sparse Core Ops, SparseCore 0:
  10.7 90.8 all-gather.2
where the time goes:
time: 328 us
  waiting for transfers between devices  251 us (77%)
  blocking collectives  39.6 us (12%)
  between operations  14 us (4%)
  matrix products  10.4 us (3%)
  starting transfers between devices  6.46 us (2%)
  other arithmetic  3.4 us (1%)
  local copies, waits for them, and re-layouts  3.29 us (1%)
    ppermute x4, waiting for transfers between devices, from_partner(): return lax.ppermute(value, axis, pairs)  199 us
    all_gather x1, waiting for transfers between devices, on_device(): lax.all_gather(out_grads, 'shard', axis=0, tiled=True)  50.8 us
    all_to_all x1, blocking collectives, on_device(): lax.all_to_all(token_acts, 'shard', split_axis=1, concat_axis=0, tiled=True)  39.6 us
    dot_general x1, matrix products, on_device(): lax.dot_general(local_cols, lax.all_gather(out_grads, 'shard', axis=0, ti...  10.4 us
  transfers between devices with their start and end apart: 5, of which 4 were waited for; matrix products, arithmetic and copies ran while one was open for 1% of the time, Pallas kernels for 0%

commit v1 on v0

v1 whole, which is shorter than its diff:
```python
import functools
import jax
import jax.numpy as jnp
from jax import lax
from jax.experimental import pallas as pl
from jax.sharding import PartitionSpec as P

step_size = 0.1
friction = 0.9
BLOCKS = (6, 10)
NODES = 16
LANES = 128
CORE_GROUPS = [[0, 2, 4, 6, 8, 10, 12, 14], [1, 3, 5, 7, 9, 11, 13, 15]]


def shard_move(value, target):
    return lax.ppermute(value, "shard", [(s, target(s)) for s in range(16)])


def other_hi(s):
    return s ^ 8


def other_core(s):
    return s ^ 1


def up_y(s):
    return (s & 9) | ((s + 2) & 6)


def down_y(s):
    return (s & 9) | ((s - 2) & 6)


def product_kernel(acts, *refs):
    grads, out = refs[:8], refs[8]
    here = lax.axis_index("shard")
    slots = [((here >> 3) ^ far) * 4 + (((here >> 1) + up) & 3) for up in (0, 3, 1, 2) for far in (0, 1)]
    lhs = jnp.concatenate([acts[slot] for slot in slots], axis=1)
    for lane in range(0, out.shape[1], 256):
        rhs = jnp.concatenate([g[:, lane : lane + 256] for g in grads], axis=0)
        out[:, lane : lane + 256] = jnp.dot(lhs, rhs, preferred_element_type=jnp.float32).astype(out.dtype)


def product(acts, grads, flip, dtype):
    rows, cols = acts.shape[1] // 2, grads[0].shape[1]
    tokens = grads[0].shape[0]

    def half_acts():
        return (0, (lax.axis_index("shard") & 1) ^ flip, 0)

    return pl.pallas_call(
        product_kernel,
        grid=(1,),
        in_specs=[pl.BlockSpec((8, rows, tokens), lambda i: half_acts())]
        + [pl.BlockSpec((tokens, cols), lambda i: (0, 0)) for _ in grads],
        out_specs=pl.BlockSpec((rows, cols), lambda i: (0, 0)),
        out_shape=jax.ShapeDtypeStruct((rows, cols), dtype),
    )(acts, *grads)


def split_rows(block, rows, per_slot):
    at, end, out = block * rows, (block + 1) * rows, []
    while at < end:
        slot = at // per_slot
        count = min(end, (slot + 1) * per_slot) - at
        out.append((slot, at - slot * per_slot, at - block * rows, count))
        at += count
    return out


def step_kernel(first, per_slot, own, other, weights, moment, new_moment, half):
    rows, cols = other.shape
    for block in range(cols // LANES):
        here = slice(block * LANES, (block + 1) * LANES)
        there = slice((first + block) * LANES, (first + block + 1) * LANES)
        for slot, to, at, count in split_rows(block, rows, per_slot):
            band = slice(at, at + count)
            grad = own[band, here] + other[band, here].astype(jnp.float32)
            moved = (friction * moment[band, there].astype(jnp.float32) + grad).astype(jnp.bfloat16)
            new_moment[band, here] = moved
            stepped = weights[band, there].astype(jnp.float32) - step_size * moved.astype(jnp.float32)
            half[slot, to : to + count] = stepped.astype(jnp.bfloat16)


def step(own, other, weights, moment, first, slot_rows):
    rows, cols = other.shape
    per_slot = rows * cols // LANES // NODES
    return pl.pallas_call(
        functools.partial(step_kernel, first, per_slot),
        out_shape=[
            jax.ShapeDtypeStruct((rows, cols), jnp.bfloat16),
            jax.ShapeDtypeStruct((NODES, slot_rows, LANES), jnp.bfloat16),
        ],
        name="step",
    )(own, other, weights, moment)


def trim_rows(halves, at, out, to, count):

    def load(r, c):
        return halves[4 * (r % 4) + c % 4, pl.ds(at, count), :].astype(jnp.float32)

    def pair(a, b):
        return a + b, jnp.maximum(a, b), jnp.minimum(a, b)

    for rp in range(2):
        for cp in range(2):
            beside = {r: pair(load(r, cp + 1), load(r, cp + 3)) for r in (rp, rp + 2)}
            above = {c: pair(load(rp + 1, c), load(rp + 3, c)) for c in (cp, cp + 2)}
            for r in (rp, rp + 2):
                for c in (cp, cp + 2):
                    mine = load(r, c)
                    row_sum, row_max, row_min = beside[r]
                    col_sum, col_max, col_min = above[c]
                    largest = jnp.maximum(jnp.maximum(row_max, col_max), mine)
                    smallest = jnp.minimum(jnp.minimum(row_min, col_min), mine)
                    total = mine + row_sum + col_sum
                    kept = (total - largest - smallest) * (1.0 / 3.0)
                    out[4 * r + c, pl.ds(to, count), :] = kept.astype(out.dtype)


def trim_kernel(rows, halves, *refs):
    out = refs[-1]
    to = out.shape[1] - rows
    if to:
        out[:, :to] = refs[0][:, :to]
    count = 8 if rows % 16 or to % 16 else 16

    def body(i, carry):
        at = pl.multiple_of(i * count, count)
        trim_rows(halves, at, out, pl.multiple_of(at + to, count), count)
        return carry

    lax.fori_loop(0, rows // count, body, 0)


def trim(halves, rows, beside):
    shape = (NODES, rows, LANES) if beside is None else beside.shape
    extra = [] if beside is None else [beside]
    return pl.pallas_call(
        functools.partial(trim_kernel, rows),
        out_shape=jax.ShapeDtypeStruct(shape, jnp.bfloat16),
        name="trim",
    )(halves, *extra)


def assemble_kernel(*refs):
    out, lane = refs[-1], 0
    for piece in refs[:-1]:
        for b in range(piece.shape[0]):
            out[:, lane : lane + LANES] = piece[b]
            lane += LANES


def assemble(pieces, shape):
    rows = shape[0] // 4
    return pl.pallas_call(
        assemble_kernel,
        grid=(4,),
        in_specs=[pl.BlockSpec((p.shape[0], rows, LANES), lambda i: (0, i, 0)) for p in pieces],
        out_specs=pl.BlockSpec((rows, shape[1]), lambda i: (i, 0)),
        out_shape=jax.ShapeDtypeStruct(shape, jnp.bfloat16),
        name="assemble",
    )(*pieces)


def node_exchange(value):
    return lax.all_to_all(value, "node", split_axis=0, concat_axis=0)


def on_device(hidden, cotangent, weights, momentum):
    acts, grads, weights, moment = hidden[0], cotangent[0], weights[0], momentum[0]
    firsts = [sum(BLOCKS[:k]) for k in range(len(BLOCKS))]
    slot_rows = [448 * b // NODES for b in BLOCKS]

    acts = acts.T.reshape(8, 896, 128)
    acts = lax.all_to_all(acts, "shard", split_axis=0, concat_axis=0, axis_index_groups=CORE_GROUPS)

    pieces = []
    for k, blocks in enumerate(BLOCKS):
        own = grads[:, firsts[k] * LANES : (firsts[k] + blocks) * LANES]
        far = shard_move(own, other_hi)
        below_own, above_own = shard_move(own, up_y), shard_move(own, down_y)
        below_far, above_far = shard_move(far, up_y), shard_move(far, down_y)
        opposite_own = shard_move(below_own, up_y)
        opposite_far = shard_move(above_far, down_y)
        pieces.append([own, far, below_own, below_far, above_own, above_far, opposite_own, opposite_far])

    moments, exchanged, back = [], None, []
    for k in range(len(BLOCKS)):
        sent = product(acts, pieces[k], 1, jnp.bfloat16)
        other = shard_move(sent, other_core)
        own = product(acts, pieces[k], 0, jnp.float32)
        rows = slot_rows[k] + (slot_rows[k - 1] if k else 0)
        new_moment, half = step(own, other, weights, moment, firsts[k], rows)
        moments.append(new_moment)
        if k:
            half = trim(exchanged, slot_rows[k - 1], half)
        exchanged = node_exchange(half)
        if k:
            back.append(exchanged[:, slot_rows[k] :])
    last = trim(exchanged, slot_rows[-1], None)
    back.append(node_exchange(last))
    new_weights = assemble([b.reshape(-1, 448, LANES) for b in back], weights.shape)
    new_moment = jnp.concatenate(moments, axis=1)
    return new_weights[None], new_moment[None]


def solution(mesh):
    spec = P("node", "shard", None)
    return jax.shard_map(on_device, mesh=mesh, in_specs=(spec,) * 4, out_specs=(spec, spec), check_vma=False)
```

time: 328 us -> 209 us (0.64)
  waiting for transfers between devices: 251 us -> 56.5 us
  starting transfers between devices: 6.46 us -> 46.2 us
  Pallas kernels: 0 us -> 37.2 us
  between operations: 14 us -> 0.85 us
  blocking collectives: 39.6 us -> 50.9 us
  local copies, waits for them, and re-layouts: 3.29 us -> 14.4 us
  matrix products: 10.4 us -> 0 us
    ppermute x4 -> x16, waiting for transfers between devices: 199 us -> 32.5 us  [shard_move(): return lax.ppermute(value, 'shard', [(s, target(s)) for s in range(16)])]
    all_gather x1 -> x0, waiting for transfers between devices: 50.8 us -> none  [on_device(): lax.all_gather(out_grads, 'shard', axis=0, tiled=True)]
    pallas_call x0 -> x9, Pallas kernels: none -> 37.2 us  [the longest x4 15.9 us: product(): pl.pallas_call(product_kernel, grid=(1,), in_specs=[pl.BlockSpec((8, rows...]
    all_to_all x0 -> x3, waiting for transfers between devices: none -> 24 us  [the longest x2 24 us: node_exchange(): return lax.all_to_all(value, 'node', split_axis=0, concat_axis=0)]
    all_to_all x0 -> x3, starting transfers between devices: none -> 21.7 us  [the longest x2 14.3 us: node_exchange(): return lax.all_to_all(value, 'node', split_axis=0, concat_axis=0)]
    ppermute x4 -> x16, starting transfers between devices: 6.42 us -> 24.5 us  [shard_move(): return lax.ppermute(value, 'shard', [(s, target(s)) for s in range(16)])]
    all_to_all x1, blocking collectives: 39.6 us -> 50.9 us  [node_exchange(): return lax.all_to_all(value, 'node', split_axis=0, concat_axis=0)]
    dot_general x1 -> x0, matrix products: 10.4 us -> none  [on_device(): lax.dot_general(local_cols, lax.all_gather(out_grads, 'shard', axis=0, ti...]
  transfers between devices with their start and end apart: 5 -> 19, of which waited for: 4 -> 6; matrix products, arithmetic and copies ran while one was open for 1% -> 3% of each run, Pallas kernels for 0% -> 12%
where the time goes in v1:
time: 209 us; the launch traced here: 207 us
  waiting for transfers between devices  56.5 us (27%)
  blocking collectives  50.9 us (24%)
  starting transfers between devices  46.2 us (22%)
  Pallas kernels  37.2 us (18%)
  local copies, waits for them, and re-layouts  14.4 us (7%)
    all_to_all x1, blocking collectives, node_exchange(): return lax.all_to_all(value, 'node', split_axis=0, concat_axis=0)  50.9 us
    ppermute x16, waiting for transfers between devices, shard_move(): return lax.ppermute(value, 'shard', [(s, target(s)) for s in range(16)])  32.5 us
    ppermute x16, starting transfers between devices, shard_move(): return lax.ppermute(value, 'shard', [(s, target(s)) for s in range(16)])  24.5 us
    all_to_all x2, waiting for transfers between devices, node_exchange(): return lax.all_to_all(value, 'node', split_axis=0, concat_axis=0)  24 us
    pallas_call x4, Pallas kernels, product(): pl.pallas_call(product_kernel, grid=(1,), in_specs=[pl.BlockSpec((8, rows...  15.9 us
    all_to_all x2, starting transfers between devices, node_exchange(): return lax.all_to_all(value, 'node', split_axis=0, concat_axis=0)  14.3 us
    pallas_call x2, Pallas kernels, step(): pl.pallas_call(functools.partial(step_kernel, first, per_slot), out_shape...  9.75 us
    pallas_call x2, Pallas kernels, trim(): pl.pallas_call(functools.partial(trim_kernel, rows), out_shape=jax.ShapeD...  7.63 us
  transfers between devices with their start and end apart: 19, of which 6 were waited for; matrix products, arithmetic and copies ran while one was open for 3% of the time, Pallas kernels for 12%

profile of v1, /device:TPU:1, one launch (start us, length us, event | category | flops | bytes accessed | tf_op | source)
XLA Modules:
  0.0 207.5 jit_solution(3325321617283719756)
XLA Ops:
  0.6 3.9 %copy.6 = bf16[7168,128]{1,0:T(8,128)(2,1)} copy(bf16[7168,128]{0,1:T(8,128)(2,1)} %bitcast.19) | data formatting | bytes 3670016 | tf_op jit(solution)/shard_map/transpose | solution.py:178
  4.5 7.5 %all-to-all-start = ((bf16[8,896,128]{2,1,0:T(8,128)(2,1)}), bf16[8,896,128]{2,1,0:T(8,128)(2,1)S(1)}, u32[]{:S(2)}, u32[]{:S(2)}) async-start(bf16[8,896,128]{2,1,0:T(8,128)(2,1)} %bitcast.12), calls=%async_computation | async-start | bytes 3670016 | tf_op jit(solution)/shard_map/all_to_all | solution.py:179
  12.0 0.9 slice.12.refs_0_
  12.9 3.1 %collective-permute-start = (bf16[128,768]{1,0:T(8,128)(2,1)S(1)}, bf16[128,768]{1,0:T(8,128)(2,1)S(1)}, u32[]{:S(2)}, u32[]{:S(2)}) collective-permute-start(bf16[128,768]{1,0:T(8,128)(2,1)S(1)} %slice.12.refs_0_), channel_id=1, source_target_pairs={{0,8},{1,9},{2,10},{3,11},{4,12},{5,13},{6,14},{7,15},{8,0},{9,1},... | collective-permute-start | bytes 589832 | tf_op jit(solution)/shard_map/ppermute | solution.py:17
  16.0 1.2 collective-permute-start.1
  17.2 21.7 %collective-permute-done.refs_1_ = bf16[128,768]{1,0:T(8,128)(2,1)S(1)} collective-permute-done((bf16[128,768]{1,0:T(8,128)(2,1)S(1)}, bf16[128,768]{1,0:T(8,128)(2,1)S(1)}, u32[]{:S(2)}, u32[]{:S(2)}) %collective-permute-start) | collective-permute-done | bytes 196640 | tf_op jit(solution)/shard_map/ppermute | solution.py:17
  38.9 2.4 %collective-permute-start.4 = (bf16[128,768]{1,0:T(8,128)(2,1)S(1)}, bf16[128,768]{1,0:T(8,128)(2,1)S(1)}, u32[]{:S(2)}, u32[]{:S(2)}) collective-permute-start(bf16[128,768]{1,0:T(8,128)(2,1)S(1)} %collective-permute-done.refs_1_), channel_id=1, source_target_pairs={{0,6},{1,7},{2,0},{3,1},{4,2},{5,3},{6,4},{7,5},{8,14},{9,15},{10,... | collective-permute-start | bytes 589832 | tf_op jit(solution)/shard_map/ppermute | solution.py:17
  41.3 0.5 collective-permute-start.3
  41.9 0.9 collective-permute-start.2
  42.8 0.0 collective-permute-done.1.refs_2_
  42.8 0.1 collective-permute-start.5
  42.9 1.1 collective-permute-done.4.refs_5_
  43.9 3.1 %collective-permute-start.6 = (bf16[128,768]{1,0:T(8,128)(2,1)S(1)}, bf16[128,768]{1,0:T(8,128)(2,1)}, u32[]{:S(2)}, u32[]{:S(2)}) collective-permute-start(bf16[128,768]{1,0:T(8,128)(2,1)S(1)} %collective-permute-done.4.refs_5_), channel_id=1, source_target_pairs={{0,6},{1,7},{2,0},{3,1},{4,2},{5,3},{6,4},{7,5},{8,14},{9,15},{10,... | collective-permute-start | bytes 589832 | tf_op jit(solution)/shard_map/ppermute | solution.py:17
  47.1 1.0 slice.13.refs_0_
  48.1 0.6 collective-permute-start.8
  48.7 0.0 collective-permute-done.3.refs_4_
  48.7 0.0 collective-permute-done.2.refs_3_
  48.7 2.6 %collective-permute-done.5.refs_6_ = bf16[128,768]{1,0:T(8,128)(2,1)S(1)} collective-permute-done((bf16[128,768]{1,0:T(8,128)(2,1)S(1)}, bf16[128,768]{1,0:T(8,128)(2,1)S(1)}, u32[]{:S(2)}, u32[]{:S(2)}) %collective-permute-start.5) | collective-permute-done | bytes 196640 | tf_op jit(solution)/shard_map/ppermute | solution.py:17
  51.3 0.7 copy-done.18
  52.0 0.6 collective-permute-done.6.refs_7_
  52.6 0.0 all-to-all-done.acts
  52.6 0.0 copy-done.4
  52.6 0.0 copy-start
  52.6 1.2 copy-done
  53.8 3.4 %shard_map.60 = bf16[448,768]{1,0:T(8,128)(2,1)} custom-call(bf16[8,896,128]{2,1,0:T(8,128)(2,1)} %copy-done, bf16[128,768]{1,0:T(8,128)(2,1)} %copy-done.4, bf16[128,768]{1,0:T(8,128)(2,1)} %copy-done.13, bf16[128,768]{1,0:T(8,128)(2,1)} %copy-done.14, bf16[128,768]{1,0:T(8,128)(2,1)} %copy-done.17, bf16[128,768]{1,0:T(8,128)(2,1)} %copy-done.16, ...), custom_call_target="tpu_custom_call" | custom-call | tf_op jit(solution)/shard_map/pallas_call | solution.py:53
  57.2 3.2 %collective-permute-start.7 = (bf16[448,768]{1,0:T(8,128)(2,1)}, bf16[448,768]{1,0:T(8,128)(2,1)S(1)}, u32[]{:S(2)}, u32[]{:S(2)}) collective-permute-start(bf16[448,768]{1,0:T(8,128)(2,1)} %shard_map.60), channel_id=1, source_target_pairs={{0,1},{1,0},{2,3},{3,2},{4,5},{5,4},{6,7},{7,6},{8,9},{9,8},{10,11... | collective-permute-start | bytes 2064392 | tf_op jit(solution)/shard_map/ppermute | solution.py:17
  60.4 0.1 collective-permute-start.9
  60.5 0.0 collective-permute-done.8.refs_1_
  60.5 3.3 %collective-permute-start.12 = (bf16[128,1280]{1,0:T(8,128)(2,1)S(1)}, bf16[128,1280]{1,0:T(8,128)(2,1)S(1)}, u32[]{:S(2)}, u32[]{:S(2)}) collective-permute-start(bf16[128,1280]{1,0:T(8,128)(2,1)S(1)} %collective-permute-done.8.refs_1_), channel_id=1, source_target_pairs={{0,6},{1,7},{2,0},{3,1},{4,2},{5,3},{6,4},{7,5},{8,14},{9,15},{10,... | collective-permute-start | bytes 983048 | tf_op jit(solution)/shard_map/ppermute | solution.py:17
  63.9 1.4 collective-permute-start.11
  65.3 0.1 collective-permute-start.10
  65.3 6.5 %collective-permute-done.9.refs_2_ = bf16[128,1280]{1,0:T(8,128)(2,1)S(1)} collective-permute-done((bf16[128,1280]{1,0:T(8,128)(2,1)S(1)}, bf16[128,1280]{1,0:T(8,128)(2,1)S(1)}, u32[]{:S(2)}, u32[]{:S(2)}) %collective-permute-start.9) | collective-permute-done | bytes 327712 | tf_op jit(solution)/shard_map/ppermute | solution.py:17
  71.9 0.0 collective-permute-start.13
  71.9 0.0 collective-permute-done.12.refs_5_
  71.9 2.7 %collective-permute-start.14 = (bf16[128,1280]{1,0:T(8,128)(2,1)S(1)}, bf16[128,1280]{1,0:T(8,128)(2,1)}, u32[]{:S(2)}, u32[]{:S(2)}) collective-permute-start(bf16[128,1280]{1,0:T(8,128)(2,1)S(1)} %collective-permute-done.12.refs_5_), channel_id=1, source_target_pairs={{0,6},{1,7},{2,0},{3,1},{4,2},{5,3},{6,4},{7,5},{8,14},{9,15},{10,... | collective-permute-start | bytes 983048 | tf_op jit(solution)/shard_map/ppermute | solution.py:17
  74.5 3.6 %shard_map.59.own = f32[448,768]{1,0:T(8,128)} custom-call(bf16[8,896,128]{2,1,0:T(8,128)(2,1)} %copy-done, bf16[128,768]{1,0:T(8,128)(2,1)} %copy-done.4, bf16[128,768]{1,0:T(8,128)(2,1)} %copy-done.13, bf16[128,768]{1,0:T(8,128)(2,1)} %copy-done.14, bf16[128,768]{1,0:T(8,128)(2,1)} %copy-done.17, bf16[128,768]{1,0:T(8,128)(2,1)} %copy-done.16, ...), custom_call_target="tpu_custom_call" | custom-call | tf_op jit(solution)/shard_map/pallas_call | solution.py:53
  78.1 0.0 collective-permute-done.7.other
  78.2 0.8 copy-done.20
  79.0 4.3 %step.2 = (bf16[448,768]{1,0:T(8,128)(2,1)}, bf16[16,168,128]{2,1,0:T(8,128)(2,1)}) custom-call(f32[448,768]{1,0:T(8,128)} %shard_map.59.own, bf16[448,768]{1,0:T(8,128)(2,1)} %copy-done.20, bf16[448,2048]{1,0:T(8,128)(2,1)} %bitcast.13, bf16[448,2048]{1,0:T(8,128)(2,1)} %bitcast.15), custom_call_target="tpu_custom_call" | custom-call | tf_op jit(solution)/shard_map/step/pallas_call | solution.py:90
  83.3 8.6 %all-to-all-start.1 = ((bf16[16,168,128]{2,1,0:T(8,128)(2,1)}), bf16[16,168,128]{2,1,0:T(8,128)(2,1)S(1)}, u32[]{:S(2)}, u32[]{:S(2)}) async-start(bf16[16,168,128]{2,1,0:T(8,128)(2,1)} %get-tuple-element.6), calls=%async_computation.1 | async-start | bytes 1376256 | tf_op jit(solution)/shard_map/all_to_all | solution.py:170
  91.8 0.0 collective-permute-done.11.refs_4_
  91.9 0.0 collective-permute-done.10.refs_3_
  91.9 0.0 collective-permute-done.13.refs_6_
  91.9 0.0 collective-permute-done.14.refs_7_
  91.9 0.7 copy-done.8
  92.6 0.1 copy-done.9
  92.7 0.1 copy-done.10
  92.8 4.3 %shard_map.62 = bf16[448,1280]{1,0:T(8,128)(2,1)} custom-call(bf16[8,896,128]{2,1,0:T(8,128)(2,1)} %copy-done, bf16[128,1280]{1,0:T(8,128)(2,1)} %copy-done.2, bf16[128,1280]{1,0:T(8,128)(2,1)} %copy-done.5, bf16[128,1280]{1,0:T(8,128)(2,1)} %copy-done.6, bf16[128,1280]{1,0:T(8,128)(2,1)} %copy-done.9, bf16[128,1280]{1,0:T(8,128)(2,1)} %copy-done.8, ...), custom_call_target="tpu_custom_call" | custom-call | tf_op jit(solution)/shard_map/pallas_call | solution.py:53
  97.1 1.7 collective-permute-start.15
  98.8 4.7 %shard_map.61.own = f32[448,1280]{1,0:T(8,128)} custom-call(bf16[8,896,128]{2,1,0:T(8,128)(2,1)} %copy-done, bf16[128,1280]{1,0:T(8,128)(2,1)} %copy-done.2, bf16[128,1280]{1,0:T(8,128)(2,1)} %copy-done.5, bf16[128,1280]{1,0:T(8,128)(2,1)} %copy-done.6, bf16[128,1280]{1,0:T(8,128)(2,1)} %copy-done.9, bf16[128,1280]{1,0:T(8,128)(2,1)} %copy-done.8, ...), custom_call_target="tpu_custom_call" | custom-call | tf_op jit(solution)/shard_map/pallas_call | solution.py:53
  103.5 0.0 collective-permute-done.15.other
  103.5 1.0 copy-done.11
  104.5 5.5 %step.3 = (bf16[448,1280]{1,0:T(8,128)(2,1)}, bf16[16,448,128]{2,1,0:T(8,128)(2,1)}) custom-call(f32[448,1280]{1,0:T(8,128)} %shard_map.61.own, bf16[448,1280]{1,0:T(8,128)(2,1)} %copy-done.11, bf16[448,2048]{1,0:T(8,128)(2,1)} %bitcast.14, bf16[448,2048]{1,0:T(8,128)(2,1)} %bitcast.16), custom_call_target="tpu_custom_call" | custom-call | tf_op jit(solution)/shard_map/step/pallas_call | solution.py:90
  110.0 0.0 all-to-all-done.1.halves
  110.0 0.8 copy-done.3
  110.9 3.8 %trim.2 = bf16[16,448,128]{2,1,0:T(8,128)(2,1)} custom-call(bf16[16,168,128]{2,1,0:T(8,128)(2,1)} %copy-done.3, bf16[16,448,128]{2,1,0:T(8,128)(2,1)} %get-tuple-element.7.refs_0_), custom_call_target="tpu_custom_call" | custom-call | tf_op jit(solution)/shard_map/trim/pallas_call | solution.py:142
  114.7 50.9 %all_to_all.20.halves = bf16[16,448,128]{2,1,0:T(8,128)(2,1)} all-to-all(bf16[16,448,128]{2,1,0:T(8,128)(2,1)} %trim.2), channel_id=1, replica_groups=mesh['node'=16,'shard'=16] {'node'}, dimensions={0} | all-to-all | bytes 3670016 | tf_op jit(solution)/shard_map/all_to_all | solution.py:170
  165.6 3.8 %trim.3 = bf16[16,280,128]{2,1,0:T(8,128)(2,1)} custom-call(bf16[16,448,128]{2,1,0:T(8,128)(2,1)} %all_to_all.20.halves), custom_call_target="tpu_custom_call" | custom-call | tf_op jit(solution)/shard_map/trim/pallas_call | solution.py:142
  169.4 5.7 %all-to-all-start.3 = ((bf16[16,280,128]{2,1,0:T(8,128)(2,1)}), bf16[16,280,128]{2,1,0:T(8,128)(2,1)S(1)}, u32[]{:S(2)}, u32[]{:S(2)}) async-start(bf16[16,280,128]{2,1,0:T(8,128)(2,1)} %trim.3), calls=%async_computation.3 | async-start | bytes 2293760 | tf_op jit(solution)/shard_map/all_to_all | solution.py:170
  175.1 1.5 maximum_bitcast_fusion
  176.6 2.0 slice.14
  178.6 24.0 %all-to-all-done.3 = bf16[16,280,128]{2,1,0:T(8,128)(2,1)S(1)} async-done(((bf16[16,280,128]{2,1,0:T(8,128)(2,1)}), bf16[16,280,128]{2,1,0:T(8,128)(2,1)S(1)}, u32[]{:S(2)}, u32[]{:S(2)}) %all-to-all-start.3) | async-done | bytes 1146912 | tf_op jit(solution)/shard_map/all_to_all | solution.py:170
  202.6 1.0 copy-done.1
  203.6 3.9 %assemble.1 = bf16[448,2048]{1,0:T(8,128)(2,1)} custom-call(bf16[6,448,128]{2,1,0:T(8,128)(2,1)} %bitcast.18, bf16[10,448,128]{2,1,0:T(8,128)(2,1)} %bitcast.17), custom_call_target="tpu_custom_call" | custom-call | tf_op jit(solution)/shard_map/assemble/pallas_call | solution.py:159
  (31 shorter events, 0.1 us)
Async XLA Ops:
  4.5 48.1 %all-to-all-start = ((bf16[8,896,128]{2,1,0:T(8,128)(2,1)}), bf16[8,896,128]{2,1,0:T(8,128)(2,1)S(1)}, u32[]{:S(2)}, u32[]{:S(2)}) async-start(bf16[8,896,128]{2,1,0:T(8,128)(2,1)} %bitcast.12), calls=%async_computation | async-start | bytes 3670016 | tf_op jit(solution)/shard_map/all_to_all | solution.py:179
  12.9 39.6 %copy-start.4 = (bf16[128,768]{1,0:T(8,128)(2,1)}, bf16[128,768]{1,0:T(8,128)(2,1)S(1)}, u32[]{:S(2)}) copy-start(bf16[128,768]{1,0:T(8,128)(2,1)S(1)} %slice.12.refs_0_) | copy-start | bytes 589828
  12.9 26.0 %collective-permute-start = (bf16[128,768]{1,0:T(8,128)(2,1)S(1)}, bf16[128,768]{1,0:T(8,128)(2,1)S(1)}, u32[]{:S(2)}, u32[]{:S(2)}) collective-permute-start(bf16[128,768]{1,0:T(8,128)(2,1)S(1)} %slice.12.refs_0_), channel_id=1, source_target_pairs={{0,8},{1,9},{2,10},{3,11},{4,12},{5,13},{6,14},{7,15},{8,0},{9,1},... | collective-permute-start | bytes 589832 | tf_op jit(solution)/shard_map/ppermute | solution.py:17
  16.0 26.8 %collective-permute-start.1 = (bf16[128,768]{1,0:T(8,128)(2,1)S(1)}, bf16[128,768]{1,0:T(8,128)(2,1)S(1)}, u32[]{:S(2)}, u32[]{:S(2)}) collective-permute-start(bf16[128,768]{1,0:T(8,128)(2,1)S(1)} %slice.12.refs_0_), channel_id=1, source_target_pairs={{0,2},{1,3},{2,4},{3,5},{4,6},{5,7},{6,0},{7,1},{8,10},{9,11},{10,... | collective-permute-start | bytes 589832 | tf_op jit(solution)/shard_map/ppermute | solution.py:17
  38.9 13.7 %copy-start.13 = (bf16[128,768]{1,0:T(8,128)(2,1)}, bf16[128,768]{1,0:T(8,128)(2,1)S(1)}, u32[]{:S(2)}) copy-start(bf16[128,768]{1,0:T(8,128)(2,1)S(1)} %collective-permute-done.refs_1_) | copy-start | bytes 589828
  38.9 5.0 %collective-permute-start.4 = (bf16[128,768]{1,0:T(8,128)(2,1)S(1)}, bf16[128,768]{1,0:T(8,128)(2,1)S(1)}, u32[]{:S(2)}, u32[]{:S(2)}) collective-permute-start(bf16[128,768]{1,0:T(8,128)(2,1)S(1)} %collective-permute-done.refs_1_), channel_id=1, source_target_pairs={{0,6},{1,7},{2,0},{3,1},{4,2},{5,3},{6,4},{7,5},{8,14},{9,15},{10,... | collective-permute-start | bytes 589832 | tf_op jit(solution)/shard_map/ppermute | solution.py:17
  41.3 7.4 %collective-permute-start.3 = (bf16[128,768]{1,0:T(8,128)(2,1)S(1)}, bf16[128,768]{1,0:T(8,128)(2,1)S(1)}, u32[]{:S(2)}, u32[]{:S(2)}) collective-permute-start(bf16[128,768]{1,0:T(8,128)(2,1)S(1)} %slice.12.refs_0_), channel_id=1, source_target_pairs={{0,6},{1,7},{2,0},{3,1},{4,2},{5,3},{6,4},{7,5},{8,14},{9,15},{10,... | collective-permute-start | bytes 589832 | tf_op jit(solution)/shard_map/ppermute | solution.py:17
  41.9 6.8 %collective-permute-start.2 = (bf16[128,768]{1,0:T(8,128)(2,1)S(1)}, bf16[128,768]{1,0:T(8,128)(2,1)S(1)}, u32[]{:S(2)}, u32[]{:S(2)}) collective-permute-start(bf16[128,768]{1,0:T(8,128)(2,1)S(1)} %collective-permute-done.refs_1_), channel_id=1, source_target_pairs={{0,2},{1,3},{2,4},{3,5},{4,6},{5,7},{6,0},{7,1},{8,10},{9,11},{10,... | collective-permute-start | bytes 589832 | tf_op jit(solution)/shard_map/ppermute | solution.py:17
  42.8 9.8 %copy-start.14 = (bf16[128,768]{1,0:T(8,128)(2,1)}, bf16[128,768]{1,0:T(8,128)(2,1)S(1)}, u32[]{:S(2)}) copy-start(bf16[128,768]{1,0:T(8,128)(2,1)S(1)} %collective-permute-done.1.refs_2_) | copy-start | bytes 589828
  42.8 8.5 %collective-permute-start.5 = (bf16[128,768]{1,0:T(8,128)(2,1)S(1)}, bf16[128,768]{1,0:T(8,128)(2,1)S(1)}, u32[]{:S(2)}, u32[]{:S(2)}) collective-permute-start(bf16[128,768]{1,0:T(8,128)(2,1)S(1)} %collective-permute-done.1.refs_2_), channel_id=1, source_target_pairs={{0,2},{1,3},{2,4},{3,5},{4,6},{5,7},{6,0},{7,1},{8,10},{9,11},{10,... | collective-permute-start | bytes 589832 | tf_op jit(solution)/shard_map/ppermute | solution.py:17
  43.9 8.6 %copy-start.15 = (bf16[128,768]{1,0:T(8,128)(2,1)}, bf16[128,768]{1,0:T(8,128)(2,1)S(1)}, u32[]{:S(2)}) copy-start(bf16[128,768]{1,0:T(8,128)(2,1)S(1)} %collective-permute-done.4.refs_5_) | copy-start | bytes 589828
  43.9 8.6 %collective-permute-start.6 = (bf16[128,768]{1,0:T(8,128)(2,1)S(1)}, bf16[128,768]{1,0:T(8,128)(2,1)}, u32[]{:S(2)}, u32[]{:S(2)}) collective-permute-start(bf16[128,768]{1,0:T(8,128)(2,1)S(1)} %collective-permute-done.4.refs_5_), channel_id=1, source_target_pairs={{0,6},{1,7},{2,0},{3,1},{4,2},{5,3},{6,4},{7,5},{8,14},{9,15},{10,... | collective-permute-start | bytes 589832 | tf_op jit(solution)/shard_map/ppermute | solution.py:17
  48.0 35.2 %copy-start.2 = (bf16[128,1280]{1,0:T(8,128)(2,1)}, bf16[128,1280]{1,0:T(8,128)(2,1)S(1)}, u32[]{:S(2)}) copy-start(bf16[128,1280]{1,0:T(8,128)(2,1)S(1)} %slice.13.refs_0_) | copy-start | bytes 983044
  48.1 12.5 %collective-permute-start.8 = (bf16[128,1280]{1,0:T(8,128)(2,1)S(1)}, bf16[128,1280]{1,0:T(8,128)(2,1)S(1)}, u32[]{:S(2)}, u32[]{:S(2)}) collective-permute-start(bf16[128,1280]{1,0:T(8,128)(2,1)S(1)} %slice.13.refs_0_), channel_id=1, source_target_pairs={{0,8},{1,9},{2,10},{3,11},{4,12},{5,13},{6,14},{7,15},{8,0},{9,1},... | collective-permute-start | bytes 983048 | tf_op jit(solution)/shard_map/ppermute | solution.py:17
  48.7 3.9 %copy-start.16 = (bf16[128,768]{1,0:T(8,128)(2,1)}, bf16[128,768]{1,0:T(8,128)(2,1)S(1)}, u32[]{:S(2)}) copy-start(bf16[128,768]{1,0:T(8,128)(2,1)S(1)} %collective-permute-done.3.refs_4_) | copy-start | bytes 589828
  48.7 2.6 %copy-start.17 = (bf16[128,768]{1,0:T(8,128)(2,1)}, bf16[128,768]{1,0:T(8,128)(2,1)S(1)}, u32[]{:S(2)}) copy-start(bf16[128,768]{1,0:T(8,128)(2,1)S(1)} %collective-permute-done.2.refs_3_) | copy-start | bytes 589828
  51.3 0.7 copy-start.18
  52.6 1.2 copy-start
  57.2 21.0 %collective-permute-start.7 = (bf16[448,768]{1,0:T(8,128)(2,1)}, bf16[448,768]{1,0:T(8,128)(2,1)S(1)}, u32[]{:S(2)}, u32[]{:S(2)}) collective-permute-start(bf16[448,768]{1,0:T(8,128)(2,1)} %shard_map.60), channel_id=1, source_target_pairs={{0,1},{1,0},{2,3},{3,2},{4,5},{5,4},{6,7},{7,6},{8,9},{9,8},{10,11... | collective-permute-start | bytes 2064392 | tf_op jit(solution)/shard_map/ppermute | solution.py:17
  60.4 11.5 %collective-permute-start.9 = (bf16[128,1280]{1,0:T(8,128)(2,1)S(1)}, bf16[128,1280]{1,0:T(8,128)(2,1)S(1)}, u32[]{:S(2)}, u32[]{:S(2)}) collective-permute-start(bf16[128,1280]{1,0:T(8,128)(2,1)S(1)} %slice.13.refs_0_), channel_id=1, source_target_pairs={{0,2},{1,3},{2,4},{3,5},{4,6},{5,7},{6,0},{7,1},{8,10},{9,11},{10,... | collective-permute-start | bytes 983048 | tf_op jit(solution)/shard_map/ppermute | solution.py:17
  60.5 17.6 %copy-start.5 = (bf16[128,1280]{1,0:T(8,128)(2,1)}, bf16[128,1280]{1,0:T(8,128)(2,1)S(1)}, u32[]{:S(2)}) copy-start(bf16[128,1280]{1,0:T(8,128)(2,1)S(1)} %collective-permute-done.8.refs_1_) | copy-start | bytes 983044
  60.5 11.4 %collective-permute-start.12 = (bf16[128,1280]{1,0:T(8,128)(2,1)S(1)}, bf16[128,1280]{1,0:T(8,128)(2,1)S(1)}, u32[]{:S(2)}, u32[]{:S(2)}) collective-permute-start(bf16[128,1280]{1,0:T(8,128)(2,1)S(1)} %collective-permute-done.8.refs_1_), channel_id=1, source_target_pairs={{0,6},{1,7},{2,0},{3,1},{4,2},{5,3},{6,4},{7,5},{8,14},{9,15},{10,... | collective-permute-start | bytes 983048 | tf_op jit(solution)/shard_map/ppermute | solution.py:17
  63.9 28.0 %collective-permute-start.11 = (bf16[128,1280]{1,0:T(8,128)(2,1)S(1)}, bf16[128,1280]{1,0:T(8,128)(2,1)S(1)}, u32[]{:S(2)}, u32[]{:S(2)}) collective-permute-start(bf16[128,1280]{1,0:T(8,128)(2,1)S(1)} %slice.13.refs_0_), channel_id=1, source_target_pairs={{0,6},{1,7},{2,0},{3,1},{4,2},{5,3},{6,4},{7,5},{8,14},{9,15},{10,... | collective-permute-start | bytes 983048 | tf_op jit(solution)/shard_map/ppermute | solution.py:17
  65.3 26.6 %collective-permute-start.10 = (bf16[128,1280]{1,0:T(8,128)(2,1)S(1)}, bf16[128,1280]{1,0:T(8,128)(2,1)S(1)}, u32[]{:S(2)}, u32[]{:S(2)}) collective-permute-start(bf16[128,1280]{1,0:T(8,128)(2,1)S(1)} %collective-permute-done.8.refs_1_), channel_id=1, source_target_pairs={{0,2},{1,3},{2,4},{3,5},{4,6},{5,7},{6,0},{7,1},{8,10},{9,11},{10,... | collective-permute-start | bytes 983048 | tf_op jit(solution)/shard_map/ppermute | solution.py:17
  71.9 6.3 %copy-start.6 = (bf16[128,1280]{1,0:T(8,128)(2,1)}, bf16[128,1280]{1,0:T(8,128)(2,1)S(1)}, u32[]{:S(2)}) copy-start(bf16[128,1280]{1,0:T(8,128)(2,1)S(1)} %collective-permute-done.9.refs_2_) | copy-start | bytes 983044
  71.9 20.0 %collective-permute-start.13 = (bf16[128,1280]{1,0:T(8,128)(2,1)S(1)}, bf16[128,1280]{1,0:T(8,128)(2,1)S(1)}, u32[]{:S(2)}, u32[]{:S(2)}) collective-permute-start(bf16[128,1280]{1,0:T(8,128)(2,1)S(1)} %collective-permute-done.9.refs_2_), channel_id=1, source_target_pairs={{0,2},{1,3},{2,4},{3,5},{4,6},{5,7},{6,0},{7,1},{8,10},{9,11},{10,... | collective-permute-start | bytes 983048 | tf_op jit(solution)/shard_map/ppermute | solution.py:17
  71.9 6.3 %copy-start.7 = (bf16[128,1280]{1,0:T(8,128)(2,1)}, bf16[128,1280]{1,0:T(8,128)(2,1)S(1)}, u32[]{:S(2)}) copy-start(bf16[128,1280]{1,0:T(8,128)(2,1)S(1)} %collective-permute-done.12.refs_5_) | copy-start | bytes 983044
  71.9 20.0 %collective-permute-start.14 = (bf16[128,1280]{1,0:T(8,128)(2,1)S(1)}, bf16[128,1280]{1,0:T(8,128)(2,1)}, u32[]{:S(2)}, u32[]{:S(2)}) collective-permute-start(bf16[128,1280]{1,0:T(8,128)(2,1)S(1)} %collective-permute-done.12.refs_5_), channel_id=1, source_target_pairs={{0,6},{1,7},{2,0},{3,1},{4,2},{5,3},{6,4},{7,5},{8,14},{9,15},{10,... | collective-permute-start | bytes 983048 | tf_op jit(solution)/shard_map/ppermute | solution.py:17
  78.1 0.8 copy-start.20
  83.3 26.8 %all-to-all-start.1 = ((bf16[16,168,128]{2,1,0:T(8,128)(2,1)}), bf16[16,168,128]{2,1,0:T(8,128)(2,1)S(1)}, u32[]{:S(2)}, u32[]{:S(2)}) async-start(bf16[16,168,128]{2,1,0:T(8,128)(2,1)} %get-tuple-element.6), calls=%async_computation.1 | async-start | bytes 1376256 | tf_op jit(solution)/shard_map/all_to_all | solution.py:170
  91.9 0.7 copy-start.8
  91.9 0.8 copy-start.9
  91.9 0.9 copy-start.10
  97.1 6.4 %collective-permute-start.15 = (bf16[448,1280]{1,0:T(8,128)(2,1)}, bf16[448,1280]{1,0:T(8,128)(2,1)S(1)}, u32[]{:S(2)}, u32[]{:S(2)}) collective-permute-start(bf16[448,1280]{1,0:T(8,128)(2,1)} %shard_map.62), channel_id=1, source_target_pairs={{0,1},{1,0},{2,3},{3,2},{4,5},{5,4},{6,7},{7,6},{8,9},{9,8},{10,11... | collective-permute-start | bytes 3440648 | tf_op jit(solution)/shard_map/ppermute | solution.py:17
  103.5 1.0 copy-start.11
  110.0 0.9 copy-start.3
  169.4 5.7 %copy-start.12 = (bf16[448,1280]{1,0:T(8,128)(2,1)S(1)}, bf16[448,1280]{1,0:T(8,128)(2,1)}, u32[]{:S(2)}) copy-start(bf16[448,1280]{1,0:T(8,128)(2,1)} %get-tuple-element.9) | copy-start | bytes 3440644
  169.4 5.7 %copy-start.19 = (bf16[448,768]{1,0:T(8,128)(2,1)S(1)}, bf16[448,768]{1,0:T(8,128)(2,1)}, u32[]{:S(2)}) copy-start(bf16[448,768]{1,0:T(8,128)(2,1)} %get-tuple-element.8) | copy-start | bytes 2064388
  169.4 33.2 %all-to-all-start.3 = ((bf16[16,280,128]{2,1,0:T(8,128)(2,1)}), bf16[16,280,128]{2,1,0:T(8,128)(2,1)S(1)}, u32[]{:S(2)}, u32[]{:S(2)}) async-start(bf16[16,280,128]{2,1,0:T(8,128)(2,1)} %trim.3), calls=%async_computation.3 | async-start | bytes 2293760 | tf_op jit(solution)/shard_map/all_to_all | solution.py:170
  202.6 1.0 copy-start.1

commit v2 on v0

v2 whole, which is shorter than its diff:
```python
import functools
import jax
import jax.numpy as jnp
from jax import lax
from jax.experimental import pallas as pl
from jax.experimental.pallas import tpu as pltpu
from jax.sharding import PartitionSpec as P

step_size = 0.1
friction = 0.9
BLOCKS = (12, 4)
NODES = 16
LANES = 128
WIDE = pltpu.CompilerParams(vmem_limit_bytes=67_000_000)
SEND_STEPS = 2
STEP_STEPS = 2
CORE_GROUPS = [[0, 2, 4, 6, 8, 10, 12, 14], [1, 3, 5, 7, 9, 11, 13, 15]]


def shard_move(value, target):
    return lax.ppermute(value, "shard", [(s, target(s)) for s in range(16)])


def other_hi(s):
    return s ^ 8


def other_core(s):
    return s ^ 1


def up_y(s):
    return (s & 9) | ((s + 2) & 6)


def down_y(s):
    return (s & 9) | ((s - 2) & 6)


def token_product(acts, grads, lane, width):
    here = lax.axis_index("shard")
    slots = [((here >> 3) ^ far) * 4 + (((here >> 1) + up) & 3) for up in (0, 3, 1, 2) for far in (0, 1)]
    lhs = jnp.concatenate([acts[slot] for slot in slots], axis=1)
    rhs = jnp.concatenate([g[:, lane : lane + width] for g in grads], axis=0)
    return jnp.dot(lhs, rhs, preferred_element_type=jnp.float32)


def half_acts(acts, flip):
    def index(i):
        return (0, (lax.axis_index("shard") & 1) ^ flip, 0)

    return pl.BlockSpec((acts.shape[0], acts.shape[1] // 2, acts.shape[2]), index)


def send_kernel(acts, *refs):
    grads, out = refs[:8], refs[8]
    for lane in range(0, out.shape[1], 256):
        out[:, lane : lane + 256] = token_product(acts, grads, lane, 256).astype(out.dtype)


def column_tile(rows, cols):
    return pl.BlockSpec((rows, cols), lambda i: (0, i))


def send_part(acts, grads):
    tokens, cols = grads[0].shape
    rows, tile = acts.shape[1] // 2, cols // SEND_STEPS
    return pl.pallas_call(
        send_kernel,
        grid=(SEND_STEPS,),
        in_specs=[half_acts(acts, 1)] + [column_tile(tokens, tile)] * 8,
        out_specs=column_tile(rows, tile),
        out_shape=jax.ShapeDtypeStruct((rows, cols), jnp.bfloat16),
        compiler_params=WIDE,
        name="send_part",
    )(acts, *grads)


def split_rows(block, rows, per_slot):
    at, end, out = block * rows, (block + 1) * rows, []
    while at < end:
        slot = at // per_slot
        count = min(end, (slot + 1) * per_slot) - at
        out.append((slot, at - slot * per_slot, at - block * rows, count))
        at += count
    return out


def spread(slots, outs):
    z = lax.axis_index("node") & 7
    for offset, out in enumerate(outs):
        out[...] = slots[(z + offset) & 7]


def step_kernel(acts, *refs):
    grads, (other, weights, moment, new_moment), rest = refs[:8], refs[8:12], refs[12:]
    half = rest[-1]
    rows, cols = other.shape
    for lane in range(0, cols, 256):
        here = slice(lane, lane + 256)
        grad = token_product(acts, grads, lane, 256) + other[:, here].astype(jnp.float32)
        moved = (friction * moment[:, here].astype(jnp.float32) + grad).astype(jnp.bfloat16)
        new_moment[:, here] = moved
        stepped = (weights[:, here].astype(jnp.float32) - step_size * moved.astype(jnp.float32)).astype(jnp.bfloat16)
        for b in range(2):
            for slot, to, at, count in split_rows(lane // LANES + b, rows, half.shape[1]):
                half[slot, to : to + count] = stepped[at : at + count, b * LANES : (b + 1) * LANES]
    if len(rest) > 1:
        spread(half, rest[:-1])


def step(acts, grads, other, weights, moment, first, apart):
    rows, cols = other.shape
    steps = 1 if apart else STEP_STEPS
    tile = cols // steps
    if first % tile:
        weights, moment, first = weights[:, first : first + cols], moment[:, first : first + cols], 0
    columns = pl.BlockSpec((rows, tile), lambda i: (0, first // tile + i))
    moved = jax.ShapeDtypeStruct((rows, cols), jnp.bfloat16)
    if apart:
        part = jax.ShapeDtypeStruct((rows * cols // LANES // 8, LANES), jnp.bfloat16)
        outs, specs = [part] * 8, [pl.BlockSpec(part.shape, lambda i: (0, 0))] * 8
        scratch = [pltpu.VMEM((8, *part.shape), jnp.bfloat16)]
    else:
        outs = [jax.ShapeDtypeStruct((cols // LANES, rows, LANES), jnp.bfloat16)]
        specs = [pl.BlockSpec((tile // LANES, rows, LANES), lambda i: (i, 0, 0))]
        scratch = []
    new_moment, *half = pl.pallas_call(
        step_kernel,
        grid=(steps,),
        in_specs=[half_acts(acts, 0)]
        + [column_tile(grads[0].shape[0], tile)] * 8
        + [column_tile(rows, tile), columns, columns],
        out_specs=[column_tile(rows, tile)] + specs,
        out_shape=[moved] + outs,
        scratch_shapes=scratch,
        compiler_params=WIDE,
        name="step",
    )(acts, *grads, other, weights, moment)
    return new_moment, half if apart else half[0].reshape(NODES, -1, LANES)


def pair(a, b):
    return a + b, jnp.maximum(a, b), jnp.minimum(a, b)


def trimmed(mine, one, two):
    one_sum, one_max, one_min = one
    two_sum, two_max, two_min = two
    largest = jnp.maximum(jnp.maximum(one_max, two_max), mine)
    smallest = jnp.minimum(jnp.minimum(one_min, two_min), mine)
    return ((mine + one_sum + two_sum - largest - smallest) * (1.0 / 3.0)).astype(jnp.bfloat16)


def over_rows(rows, body):
    count = 8 if rows % 16 else 16

    def one(i, carry):
        body(pl.ds(pl.multiple_of(i * count, count), count))
        return carry

    lax.fori_loop(0, rows // count, one, 0)


def trim_kernel(halves, out):
    def body(at):
        def load(r, c):
            return halves[4 * (r % 4) + c % 4, at, :].astype(jnp.float32)

        for rp in range(2):
            for cp in range(2):
                beside = {r: pair(load(r, cp + 1), load(r, cp + 3)) for r in (rp, rp + 2)}
                above = {c: pair(load(rp + 1, c), load(rp + 3, c)) for c in (cp, cp + 2)}
                for r in (rp, rp + 2):
                    for c in (cp, cp + 2):
                        out[4 * r + c, at, :] = trimmed(load(r, c), beside[r], above[c])

    over_rows(halves.shape[1], body)


def trim(halves):
    tile = halves.shape[1] if halves.shape[1] % 112 else 112
    spec = pl.BlockSpec((NODES, tile, LANES), lambda i: (0, i, 0))
    return pl.pallas_call(
        trim_kernel,
        grid=(halves.shape[1] // tile,),
        in_specs=[spec],
        out_specs=spec,
        out_shape=jax.ShapeDtypeStruct(halves.shape, jnp.bfloat16),
        compiler_params=WIDE,
        name="trim",
    )(halves)


def trim_apart_kernel(*refs):
    outs, (near, far, result) = refs[16:24], refs[24:]
    z = lax.axis_index("node") & 7
    for offset in range(8):
        near[(z - offset) & 7] = refs[offset][...]
        far[(z - offset) & 7] = refs[8 + offset][...]

    def body(at):
        def load(ref, r, c):
            return ref[4 * r + c % 4, at, :].astype(jnp.float32)

        for r in range(2):
            for cp in range(2):
                beside = pair(load(near, r, cp + 1), load(near, r, cp + 3))
                for c in (cp, cp + 2):
                    above = pair(load(near, 1 - r, c), load(far, 1 - r, c))
                    result[4 * r + c, at, :] = trimmed(load(near, r, c), beside, above)

    over_rows(near.shape[1], body)
    spread(result, outs)


def trim_apart(near, far):
    rows = near[0].shape[0]
    tile = 112 if rows % 224 else 224
    out = jax.ShapeDtypeStruct((rows, LANES), jnp.bfloat16)
    spec = pl.BlockSpec((tile, LANES), lambda i: (i, 0))
    return pl.pallas_call(
        trim_apart_kernel,
        grid=(rows // tile,),
        in_specs=[spec] * 16,
        out_specs=[spec] * 8,
        out_shape=[out] * 8,
        scratch_shapes=[pltpu.VMEM((8, tile, LANES), jnp.bfloat16)] * 3,
        compiler_params=WIDE,
        name="trim_apart",
    )(*near, *far)


ANY = pl.BlockSpec(memory_space=pl.ANY)


def copy_all(pairs, sems):
    copies = [pltpu.make_async_copy(source, target, sems.at[i]) for i, (source, target) in enumerate(pairs)]
    for copy in copies:
        copy.start()
    for copy in copies:
        copy.wait()


def lay_kernel(piece, out, sems):
    copy_all([(piece.at[b], out.at[:, pl.ds(b * LANES, LANES)]) for b in range(piece.shape[0])], sems)


def lay(piece, shape):
    return pl.pallas_call(
        lay_kernel,
        in_specs=[pl.BlockSpec(memory_space=pltpu.VMEM)],
        out_specs=ANY,
        out_shape=jax.ShapeDtypeStruct(shape, jnp.bfloat16),
        scratch_shapes=[pltpu.SemaphoreType.DMA((piece.shape[0],))],
        compiler_params=WIDE,
        name="lay",
    )(piece)


def lay_apart_kernel(first, laid, *refs):
    del laid
    pieces, out, sems = refs[:8], refs[8], refs[9]
    z = lax.axis_index("node") & 7
    parts = pieces[0].shape[0] // 112
    pairs = []
    for offset, piece in enumerate(pieces):
        for part in range(parts):
            spot = ((z - offset) & 7) * parts + part
            lane = pl.multiple_of((first + (spot >> 2)) * LANES, LANES)
            row = pl.multiple_of((spot & 3) * 112, 16)
            pairs.append((piece.at[pl.ds(part * 112, 112)], out.at[pl.ds(row, 112), pl.ds(lane, LANES)]))
    copy_all(pairs, sems)


def lay_apart(laid, pieces, first):
    return pl.pallas_call(
        functools.partial(lay_apart_kernel, first),
        in_specs=[ANY] + [pl.BlockSpec(memory_space=pltpu.VMEM)] * 8,
        out_specs=ANY,
        out_shape=jax.ShapeDtypeStruct(laid.shape, jnp.bfloat16),
        scratch_shapes=[pltpu.SemaphoreType.DMA((8 * pieces[0].shape[0] // 112,))],
        input_output_aliases={0: 0},
        compiler_params=WIDE,
        name="lay_apart",
    )(laid, *pieces)


ORDER = (4, 5, 3, 6, 2, 7, 1)


def ring_exchange(pieces):
    got = {0: pieces[0]}
    for offset in ORDER:
        pairs = [(n, (n & 8) | ((n + offset) & 7)) for n in range(NODES)]
        got[offset] = lax.ppermute(pieces[offset], "node", pairs)
    return [got[offset] for offset in range(8)]


def node_exchange(value):
    return lax.all_to_all(value, "node", split_axis=0, concat_axis=0)


def on_device(hidden, cotangent, weights, momentum):
    acts, grads, weights, moment = hidden[0], cotangent[0], weights[0], momentum[0]
    cuts = [slice(0, BLOCKS[0] * LANES), slice(BLOCKS[0] * LANES, grads.shape[1])]

    acts = acts.T.reshape(8, 896, 128)
    acts = lax.all_to_all(acts, "shard", split_axis=0, concat_axis=0, axis_index_groups=CORE_GROUPS)

    pieces = []
    for cut in cuts:
        own = grads[:, cut]
        far = shard_move(own, other_hi)
        below_own, above_own = shard_move(own, up_y), shard_move(own, down_y)
        below_far, above_far = shard_move(far, up_y), shard_move(far, down_y)
        opposite_own = shard_move(below_own, up_y)
        opposite_far = shard_move(above_far, down_y)
        pieces.append([own, far, below_own, below_far, above_own, above_far, opposite_own, opposite_far])

    moments, halves = [], []
    for k, cut in enumerate(cuts):
        sent = send_part(acts, pieces[k])
        other = shard_move(sent, other_core)
        new_moment, half = step(acts, pieces[k], other, weights, moment, cut.start, k == 1)
        moments.append(new_moment)
        halves.append(half)

    exchanged = node_exchange(halves[0])
    result = trim(exchanged)
    returned = node_exchange(result)
    laid = lay(returned.reshape(-1, 448, LANES), weights.shape)

    near = ring_exchange(halves[1])
    far = []
    for piece in near:
        far.append(lax.ppermute(piece, "node", [(n, n ^ 8) for n in range(NODES)]))
    results = trim_apart(near, far)
    arrived = ring_exchange(results)
    new_weights = lay_apart(laid, arrived, BLOCKS[0])
    new_moment = jnp.concatenate(moments, axis=1)
    return new_weights[None], new_moment[None]


def solution(mesh):
    spec = P("node", "shard", None)
    return jax.shard_map(on_device, mesh=mesh, in_specs=(spec,) * 4, out_specs=(spec, spec), check_vma=False)
```

time: 328 us -> 225 us (0.69)
  waiting for transfers between devices: 251 us -> 63.9 us
  starting transfers between devices: 6.46 us -> 78 us
  Pallas kernels: 0 us -> 27.9 us
  between operations: 14 us -> 1.04 us
  matrix products: 10.4 us -> 0 us
  local copies, waits for them, and re-layouts: 3.29 us -> 6.9 us
    ppermute x4 -> x38, waiting for transfers between devices: 199 us -> 63.9 us  [the longest x16 57.5 us: shard_move(): return lax.ppermute(value, 'shard', [(s, target(s)) for s in range(16)])]
    ppermute x4 -> x38, starting transfers between devices: 6.42 us -> 64.8 us  [the longest x16 28.7 us: shard_move(): return lax.ppermute(value, 'shard', [(s, target(s)) for s in range(16)])]
    all_gather x1 -> x0, waiting for transfers between devices: 50.8 us -> none  [on_device(): lax.all_gather(out_grads, 'shard', axis=0, tiled=True)]
    pallas_call x0 -> x8, Pallas kernels: none -> 27.9 us  [the longest x2 9.34 us: step(): pl.pallas_call(step_kernel, grid=(steps,), in_specs=[half_acts(acts, 0)]...]
    all_to_all x0 -> x2, starting transfers between devices: none -> 13.3 us  [the longest x1 7.6 us: on_device(): lax.all_to_all(acts, 'shard', split_axis=0, concat_axis=0, axis_index_gro...]
    dot_general x1 -> x0, matrix products: 10.4 us -> none  [on_device(): lax.dot_general(local_cols, lax.all_gather(out_grads, 'shard', axis=0, ti...]
    transpose x0 -> x1, local copies, waits for them, and re-layouts: none -> 3.88 us  [on_device(): acts = acts.T.reshape(8, 896, 128)]
  transfers between devices with their start and end apart: 5 -> 40, of which waited for: 4 -> 18; matrix products, arithmetic and copies ran while one was open for 1% -> 2% of each run, Pallas kernels for 0% -> 5%
where the time goes in v2:
time: 225 us; the launch traced here: 222 us
  starting transfers between devices  78 us (35%)
  waiting for transfers between devices  63.9 us (28%)
  blocking collectives  41.4 us (18%)
  Pallas kernels  27.9 us (12%)
  local copies, waits for them, and re-layouts  6.9 us (3%)
  other arithmetic  2.97 us (1%)
    ppermute x16, waiting for transfers between devices, shard_move(): return lax.ppermute(value, 'shard', [(s, target(s)) for s in range(16)])  57.5 us
    all_to_all x1, blocking collectives, node_exchange(): return lax.all_to_all(value, 'node', split_axis=0, concat_axis=0)  41.4 us
    ppermute x16, starting transfers between devices, shard_move(): return lax.ppermute(value, 'shard', [(s, target(s)) for s in range(16)])  28.7 us
    ppermute x14, starting transfers between devices, ring_exchange(): got[offset] = lax.ppermute(pieces[offset], 'node', pairs)  27.7 us
    pallas_call x2, Pallas kernels, step(): pl.pallas_call(step_kernel, grid=(steps,), in_specs=[half_acts(acts, 0)]...  9.34 us
    ppermute x8, starting transfers between devices, on_device(): far.append(lax.ppermute(piece, 'node', [(n, n ^ 8) for n in range(NODES)]))  8.41 us
    all_to_all x1, starting transfers between devices, on_device(): lax.all_to_all(acts, 'shard', split_axis=0, concat_axis=0, axis_index_gro...  7.6 us
    pallas_call x2, Pallas kernels, send_part(): pl.pallas_call(send_kernel, grid=(SEND_STEPS,), in_specs=[half_acts(acts,...  7.53 us
  transfers between devices with their start and end apart: 40, of which 18 were waited for; matrix products, arithmetic and copies ran while one was open for 2% of the time, Pallas kernels for 5%

profile of v2, /device:TPU:1, one launch (start us, length us, event | category | flops | bytes accessed | tf_op | source)
XLA Modules:
  0.0 222.1 jit_solution(13269655222823163530)
XLA Ops:
  0.6 3.9 %copy.7 = bf16[7168,128]{1,0:T(8,128)(2,1)} copy(bf16[7168,128]{0,1:T(8,128)(2,1)} %bitcast.17) | data formatting | bytes 3670016 | tf_op jit(solution)/shard_map/transpose | solution.py:308
  4.5 7.6 %all-to-all-start = ((bf16[8,896,128]{2,1,0:T(8,128)(2,1)}), bf16[8,896,128]{2,1,0:T(8,128)(2,1)}, u32[]{:S(2)}, u32[]{:S(2)}) async-start(bf16[8,896,128]{2,1,0:T(8,128)(2,1)} %bitcast.2), calls=%async_computation | async-start | bytes 3670016 | tf_op jit(solution)/shard_map/all_to_all | solution.py:309
  12.2 3.0 %collective-permute-start = (bf16[128,1536]{1,0:T(8,128)(2,1)S(1)}, bf16[128,1536]{1,0:T(8,128)(2,1)S(1)}, u32[]{:S(2)}, u32[]{:S(2)}) collective-permute-start(bf16[128,1536]{1,0:T(8,128)(2,1)S(1)} %slice.8.refs_0_), channel_id=1, source_target_pairs={{0,8},{1,9},{2,10},{3,11},{4,12},{5,13},{6,14},{7,15},{8,0},{9,1},... | collective-permute-start | bytes 1179656 | tf_op jit(solution)/shard_map/ppermute | solution.py:21
  15.2 1.2 collective-permute-start.1
  16.4 26.8 %collective-permute-done.refs_1_ = bf16[128,1536]{1,0:T(8,128)(2,1)S(1)} collective-permute-done((bf16[128,1536]{1,0:T(8,128)(2,1)S(1)}, bf16[128,1536]{1,0:T(8,128)(2,1)S(1)}, u32[]{:S(2)}, u32[]{:S(2)}) %collective-permute-start) | collective-permute-done | bytes 393248 | tf_op jit(solution)/shard_map/ppermute | solution.py:21
  43.2 2.4 %collective-permute-start.4 = (bf16[128,1536]{1,0:T(8,128)(2,1)S(1)}, bf16[128,1536]{1,0:T(8,128)(2,1)S(1)}, u32[]{:S(2)}, u32[]{:S(2)}) collective-permute-start(bf16[128,1536]{1,0:T(8,128)(2,1)S(1)} %collective-permute-done.refs_1_), channel_id=1, source_target_pairs={{0,6},{1,7},{2,0},{3,1},{4,2},{5,3},{6,4},{7,5},{8,14},{9,15},{10,... | collective-permute-start | bytes 1179656 | tf_op jit(solution)/shard_map/ppermute | solution.py:21
  45.7 0.5 collective-permute-start.3
  46.2 0.9 collective-permute-start.2
  47.2 5.1 %collective-permute-done.4.refs_5_ = bf16[128,1536]{1,0:T(8,128)(2,1)S(1)} collective-permute-done((bf16[128,1536]{1,0:T(8,128)(2,1)S(1)}, bf16[128,1536]{1,0:T(8,128)(2,1)S(1)}, u32[]{:S(2)}, u32[]{:S(2)}) %collective-permute-start.4) | collective-permute-done | bytes 393248 | tf_op jit(solution)/shard_map/ppermute | solution.py:21
  52.3 3.4 %collective-permute-start.6 = (bf16[128,1536]{1,0:T(8,128)(2,1)S(1)}, bf16[128,1536]{1,0:T(8,128)(2,1)}, u32[]{:S(2)}, u32[]{:S(2)}) collective-permute-start(bf16[128,1536]{1,0:T(8,128)(2,1)S(1)} %collective-permute-done.4.refs_5_), channel_id=1, source_target_pairs={{0,6},{1,7},{2,0},{3,1},{4,2},{5,3},{6,4},{7,5},{8,14},{9,15},{10,... | collective-permute-start | bytes 1179656 | tf_op jit(solution)/shard_map/ppermute | solution.py:21
  55.7 5.0 %collective-permute-done.3.refs_4_ = bf16[128,1536]{1,0:T(8,128)(2,1)S(1)} collective-permute-done((bf16[128,1536]{1,0:T(8,128)(2,1)S(1)}, bf16[128,1536]{1,0:T(8,128)(2,1)S(1)}, u32[]{:S(2)}, u32[]{:S(2)}) %collective-permute-start.3) | collective-permute-done | bytes 393248 | tf_op jit(solution)/shard_map/ppermute | solution.py:21
  60.7 3.4 %collective-permute-done.5.refs_6_ = bf16[128,1536]{1,0:T(8,128)(2,1)S(1)} collective-permute-done((bf16[128,1536]{1,0:T(8,128)(2,1)S(1)}, bf16[128,1536]{1,0:T(8,128)(2,1)S(1)}, u32[]{:S(2)}, u32[]{:S(2)}) %collective-permute-start.5) | collective-permute-done | bytes 393248 | tf_op jit(solution)/shard_map/ppermute | solution.py:21
  64.1 0.7 copy-done.6
  64.8 4.3 %collective-permute-done.6.refs_7_ = bf16[128,1536]{1,0:T(8,128)(2,1)} collective-permute-done((bf16[128,1536]{1,0:T(8,128)(2,1)S(1)}, bf16[128,1536]{1,0:T(8,128)(2,1)}, u32[]{:S(2)}, u32[]{:S(2)}) %collective-permute-start.6) | collective-permute-done | bytes 393248 | tf_op jit(solution)/shard_map/ppermute | solution.py:21
  69.1 4.5 %send_part.2 = bf16[448,1536]{1,0:T(8,128)(2,1)} custom-call(bf16[8,896,128]{2,1,0:T(8,128)(2,1)} %all-to-all-done.acts, bf16[128,1536]{1,0:T(8,128)(2,1)} %copy-done, bf16[128,1536]{1,0:T(8,128)(2,1)} %copy-done.1, bf16[128,1536]{1,0:T(8,128)(2,1)} %copy-done.2, bf16[128,1536]{1,0:T(8,128)(2,1)} %copy-done.5, bf16[128,1536]{1,0:T(8,128)(2,1)} %copy-done.4, ...), custom_call_target="tpu_custom_call" | custom-call | tf_op jit(solution)/shard_map/send_part/pallas_call | solution.py:68
  73.6 2.7 %collective-permute-start.7 = (bf16[448,1536]{1,0:T(8,128)(2,1)}, bf16[448,1536]{1,0:T(8,128)(2,1)}, u32[]{:S(2)}, u32[]{:S(2)}) collective-permute-start(bf16[448,1536]{1,0:T(8,128)(2,1)} %send_part.2), channel_id=1, source_target_pairs={{0,1},{1,0},{2,3},{3,2},{4,5},{5,4},{6,7},{7,6},{8,9},{9,8},{10,11... | collective-permute-start | bytes 4128776 | tf_op jit(solution)/shard_map/ppermute | solution.py:21
  76.3 3.1 %collective-permute-done.7.refs_8_ = bf16[448,1536]{1,0:T(8,128)(2,1)} collective-permute-done((bf16[448,1536]{1,0:T(8,128)(2,1)}, bf16[448,1536]{1,0:T(8,128)(2,1)}, u32[]{:S(2)}, u32[]{:S(2)}) %collective-permute-start.7) | collective-permute-done | bytes 1376288 | tf_op jit(solution)/shard_map/ppermute | solution.py:21
  79.4 5.7 %step.2 = (bf16[448,1536]{1,0:T(8,128)(2,1)}, bf16[12,448,128]{2,1,0:T(8,128)(2,1)}) custom-call(bf16[8,896,128]{2,1,0:T(8,128)(2,1)} %all-to-all-done.acts, bf16[128,1536]{1,0:T(8,128)(2,1)} %copy-done, bf16[128,1536]{1,0:T(8,128)(2,1)} %copy-done.1, bf16[128,1536]{1,0:T(8,128)(2,1)} %copy-done.2, bf16[128,1536]{1,0:T(8,128)(2,1)} %copy-done.5, ...), custom_call_target="tpu_custom_call" | custom-call | tf_op jit(solution)/shard_map/step/pallas_call | solution.py:128
  85.2 41.4 %all_to_all.15.halves = bf16[16,336,128]{2,1,0:T(8,128)(2,1)} all-to-all(bf16[16,336,128]{2,1,0:T(8,128)(2,1)} %bitcast.18), channel_id=1, replica_groups=mesh['node'=16,'shard'=16] {'node'}, dimensions={0} | all-to-all | bytes 2752512 | tf_op jit(solution)/shard_map/all_to_all | solution.py:301
  126.6 3.9 %trim.1 = bf16[16,336,128]{2,1,0:T(8,128)(2,1)} custom-call(bf16[16,336,128]{2,1,0:T(8,128)(2,1)} %all_to_all.15.halves), custom_call_target="tpu_custom_call" | custom-call | tf_op jit(solution)/shard_map/trim/pallas_call | solution.py:184
  130.5 5.7 %all-to-all-start.2 = ((bf16[16,336,128]{2,1,0:T(8,128)(2,1)}), bf16[16,336,128]{2,1,0:T(8,128)(2,1)}, u32[]{:S(2)}, u32[]{:S(2)}) async-start(bf16[16,336,128]{2,1,0:T(8,128)(2,1)} %trim.1), calls=%async_computation.2 | async-start | bytes 2752512 | tf_op jit(solution)/shard_map/all_to_all | solution.py:301
  136.2 0.9 slice.9.refs_0_
  137.1 0.7 collective-permute-start.8
  137.8 1.0 collective-permute-start.9
  138.9 6.0 %collective-permute-done.8.refs_1_ = bf16[128,512]{1,0:T(8,128)(2,1)S(1)} collective-permute-done((bf16[128,512]{1,0:T(8,128)(2,1)S(1)}, bf16[128,512]{1,0:T(8,128)(2,1)S(1)}, u32[]{:S(2)}, u32[]{:S(2)}) %collective-permute-start.8) | collective-permute-done | bytes 131104 | tf_op jit(solution)/shard_map/ppermute | solution.py:21
  144.9 3.6 %collective-permute-start.12 = (bf16[128,512]{1,0:T(8,128)(2,1)S(1)}, bf16[128,512]{1,0:T(8,128)(2,1)S(1)}, u32[]{:S(2)}, u32[]{:S(2)}) collective-permute-start(bf16[128,512]{1,0:T(8,128)(2,1)S(1)} %collective-permute-done.8.refs_1_), channel_id=1, source_target_pairs={{0,6},{1,7},{2,0},{3,1},{4,2},{5,3},{6,4},{7,5},{8,14},{9,15},{10,... | collective-permute-start | bytes 393224 | tf_op jit(solution)/shard_map/ppermute | solution.py:21
  148.5 1.4 collective-permute-start.10
  149.9 0.3 collective-permute-start.13
  150.4 3.3 %collective-permute-start.14 = (bf16[128,512]{1,0:T(8,128)(2,1)S(1)}, bf16[128,512]{1,0:T(8,128)(2,1)}, u32[]{:S(2)}, u32[]{:S(2)}) collective-permute-start(bf16[128,512]{1,0:T(8,128)(2,1)S(1)} %collective-permute-done.12.refs_5_), channel_id=1, source_target_pairs={{0,6},{1,7},{2,0},{3,1},{4,2},{5,3},{6,4},{7,5},{8,14},{9,15},{10,... | collective-permute-start | bytes 393224 | tf_op jit(solution)/shard_map/ppermute | solution.py:21
  153.7 0.2 collective-permute-done.10.refs_3_
  154.0 1.4 collective-permute-done.13.refs_6_
  155.4 0.6 copy-done.13
  156.2 3.0 %send_part.3 = bf16[448,512]{1,0:T(8,128)(2,1)} custom-call(bf16[8,896,128]{2,1,0:T(8,128)(2,1)} %all-to-all-done.acts, bf16[128,512]{1,0:T(8,128)(2,1)} %copy-done.7, bf16[128,512]{1,0:T(8,128)(2,1)} %copy-done.8, bf16[128,512]{1,0:T(8,128)(2,1)} %copy-done.9, bf16[128,512]{1,0:T(8,128)(2,1)} %copy-done.12, bf16[128,512]{1,0:T(8,128)(2,1)} %copy-done.11, ...), custom_call_target="tpu_custom_call" | custom-call | tf_op jit(solution)/shard_map/send_part/pallas_call | solution.py:68
  159.2 4.0 %collective-permute-start.15 = (bf16[448,512]{1,0:T(8,128)(2,1)}, bf16[448,512]{1,0:T(8,128)(2,1)}, u32[]{:S(2)}, u32[]{:S(2)}) collective-permute-start(bf16[448,512]{1,0:T(8,128)(2,1)} %send_part.3), channel_id=1, source_target_pairs={{0,1},{1,0},{2,3},{3,2},{4,5},{5,4},{6,7},{7,6},{8,9},{9,8},{10,11... | collective-permute-start | bytes 1376264 | tf_op jit(solution)/shard_map/ppermute | solution.py:21
  163.2 1.8 collective-permute-done.15.refs_8_
  165.0 3.6 %step.3 = (bf16[448,512]{1,0:T(8,128)(2,1)}, bf16[224,128]{1,0:T(8,128)(2,1)}, bf16[224,128]{1,0:T(8,128)(2,1)}, bf16[224,128]{1,0:T(8,128)(2,1)}, bf16[224,128]...) custom-call(bf16[8,896,128]{2,1,0:T(8,128)(2,1)} %all-to-all-done.ac, ...), custom_call_target="tpu_custom_call" | custom-call | tf_op jit(solution)/shard_map/step/pallas_call | solution.py:128
  168.6 0.9 collective-permute-start.16
  169.5 4.4 %collective-permute-start.17 = (bf16[224,128]{1,0:T(8,128)(2,1)}, bf16[224,128]{1,0:T(8,128)(2,1)S(1)}, u32[]{:S(2)}, u32[]{:S(2)}) collective-permute-start(bf16[224,128]{1,0:T(8,128)(2,1)} %get-tuple-element.24), channel_id=1, source_target_pairs={{0,32},{16,48},{32,64},{48,80},{64,96},{80,112},{96,0},{112,16},{1... | collective-permute-start | bytes 172040 | tf_op jit(solution)/shard_map/ppermute | solution.py:296
  173.9 1.3 collective-permute-start.18
  175.1 4.3 %collective-permute-start.19 = (bf16[224,128]{1,0:T(8,128)(2,1)}, bf16[224,128]{1,0:T(8,128)(2,1)S(1)}, u32[]{:S(2)}, u32[]{:S(2)}) collective-permute-start(bf16[224,128]{1,0:T(8,128)(2,1)} %get-tuple-element.26), channel_id=1, source_target_pairs={{0,64},{16,80},{32,96},{48,112},{64,0},{80,16},{96,32},{112,48},{1... | collective-permute-start | bytes 172040 | tf_op jit(solution)/shard_map/ppermute | solution.py:296
  179.6 3.4 %collective-permute-start.21 = (bf16[224,128]{1,0:T(8,128)(2,1)}, bf16[224,128]{1,0:T(8,128)(2,1)S(1)}, u32[]{:S(2)}, u32[]{:S(2)}) collective-permute-start(bf16[224,128]{1,0:T(8,128)(2,1)} %get-tuple-element.28), channel_id=1, source_target_pairs={{0,96},{16,112},{32,0},{48,16},{64,32},{80,48},{96,64},{112,80},{1... | collective-permute-start | bytes 172040 | tf_op jit(solution)/shard_map/ppermute | solution.py:296
  183.0 1.4 collective-permute-start.22
  184.4 1.5 collective-permute-start.23
  185.9 1.2 collective-permute-start.24
  187.0 0.6 collective-permute-start.25
  187.7 2.4 %collective-permute-done.21.refs_6_ = bf16[224,128]{1,0:T(8,128)(2,1)S(1)} collective-permute-done((bf16[224,128]{1,0:T(8,128)(2,1)}, bf16[224,128]{1,0:T(8,128)(2,1)S(1)}, u32[]{:S(2)}, u32[]{:S(2)}) %collective-permute-start.21) | collective-permute-done | bytes 57376 | tf_op jit(solution)/shard_map/ppermute | solution.py:296
  190.1 1.8 collective-permute-start.26
  192.0 1.4 collective-permute-start.28
  193.6 1.7 collective-permute-start.30
  195.3 0.7 collective-permute-done.28.refs_13_
  196.0 1.4 collective-permute-done.29.refs_14_
  197.4 0.6 copy-done.28
  198.1 0.6 collective-permute-done.30.refs_15_
  198.6 2.7 %trim_apart.1 = (bf16[224,128]{1,0:T(8,128)(2,1)}, bf16[224,128]{1,0:T(8,128)(2,1)}, bf16[224,128]{1,0:T(8,128)(2,1)}, bf16[224,128]{1,0:T(8,128)(2,1)}, bf16[22...) custom-call(bf16[224,128]{1,0:T(8,128)(2,1)} %get-tuple-element.22.refs_0_, ...), custom_call_target="tpu_custom_call" | custom-call | tf_op jit(solution)/shard_map/trim_apart/pallas_call | solution.py:222
  201.3 1.3 collective-permute-start.31
  202.6 3.2 %collective-permute-start.33 = (bf16[224,128]{1,0:T(8,128)(2,1)}, bf16[224,128]{1,0:T(8,128)(2,1)}, u32[]{:S(2)}, u32[]{:S(2)}) collective-permute-start(bf16[224,128]{1,0:T(8,128)(2,1)} %get-tuple-element.33), channel_id=1, source_target_pairs={{0,48},{16,64},{32,80},{48,96},{64,112},{80,0},{96,16},{112,32},{1... | collective-permute-start | bytes 172040 | tf_op jit(solution)/shard_map/ppermute | solution.py:296
  205.8 2.2 %collective-permute-start.34 = (bf16[224,128]{1,0:T(8,128)(2,1)}, bf16[224,128]{1,0:T(8,128)(2,1)}, u32[]{:S(2)}, u32[]{:S(2)}) collective-permute-start(bf16[224,128]{1,0:T(8,128)(2,1)} %get-tuple-element.34), channel_id=1, source_target_pairs={{0,64},{16,80},{32,96},{48,112},{64,0},{80,16},{96,32},{112,48},{1... | collective-permute-start | bytes 172040 | tf_op jit(solution)/shard_map/ppermute | solution.py:296
  208.0 3.2 %collective-permute-start.35 = (bf16[224,128]{1,0:T(8,128)(2,1)}, bf16[224,128]{1,0:T(8,128)(2,1)}, u32[]{:S(2)}, u32[]{:S(2)}) collective-permute-start(bf16[224,128]{1,0:T(8,128)(2,1)} %get-tuple-element.35), channel_id=1, source_target_pairs={{0,80},{16,96},{32,112},{48,0},{64,16},{80,32},{96,48},{112,64},{1... | collective-permute-start | bytes 172040 | tf_op jit(solution)/shard_map/ppermute | solution.py:296
  211.2 2.0 collective-permute-start.36
  213.2 3.0 %maximum_bitcast_fusion = bf16[1,448,2048]{2,1,0:T(8,128)(2,1)} fusion(bf16[448,512]{1,0:T(8,128)(2,1)} %get-tuple-element.39, bf16[448,1536]{1,0:T(8,128)(2,1)} %get-tuple-element.38), kind=kLoop, calls=%fused_computation | loop fusion | flops 3670016 | bytes 3670016 | tf_op jit(solution)/shard_map/broadcast_in_dim | solution.py:342
  216.2 2.5 %lay.1.laid = bf16[448,2048]{1,0:T(8,128)(2,1)} custom-call(bf16[12,448,128]{2,1,0:T(8,128)(2,1)} %bitcast.7.piece), custom_call_target="tpu_custom_call" | custom-call | tf_op jit(solution)/shard_map/lay/pallas_call | solution.py:250
  218.7 0.5 collective-permute-done.36.refs_6_
  219.2 0.8 collective-permute-done.37.refs_7_
  220.0 1.9 lay_apart.1
  (87 shorter events, 1.2 us)
Async XLA Ops:
  4.5 7.6 %copy-start.14 = (bf16[1,128,2048]{2,1,0:T(8,128)(2,1)S(1)}, bf16[1,128,2048]{2,1,0:T(8,128)(2,1)}, u32[]{:S(2)}) copy-start(bf16[1,128,2048]{2,1,0:T(8,128)(2,1)} %param.5) | copy-start | bytes 1572868
  4.5 64.6 %all-to-all-start = ((bf16[8,896,128]{2,1,0:T(8,128)(2,1)}), bf16[8,896,128]{2,1,0:T(8,128)(2,1)}, u32[]{:S(2)}, u32[]{:S(2)}) async-start(bf16[8,896,128]{2,1,0:T(8,128)(2,1)} %bitcast.2), calls=%async_computation | async-start | bytes 3670016 | tf_op jit(solution)/shard_map/all_to_all | solution.py:309
  12.1 33.5 %copy-start = (bf16[128,1536]{1,0:T(8,128)(2,1)}, bf16[128,1536]{1,0:T(8,128)(2,1)S(1)}, u32[]{:S(2)}) copy-start(bf16[128,1536]{1,0:T(8,128)(2,1)S(1)} %slice.8.refs_0_) | copy-start | bytes 1179652
  12.2 31.1 %collective-permute-start = (bf16[128,1536]{1,0:T(8,128)(2,1)S(1)}, bf16[128,1536]{1,0:T(8,128)(2,1)S(1)}, u32[]{:S(2)}, u32[]{:S(2)}) collective-permute-start(bf16[128,1536]{1,0:T(8,128)(2,1)S(1)} %slice.8.refs_0_), channel_id=1, source_target_pairs={{0,8},{1,9},{2,10},{3,11},{4,12},{5,13},{6,14},{7,15},{8,0},{9,1},... | collective-permute-start | bytes 1179656 | tf_op jit(solution)/shard_map/ppermute | solution.py:21
  15.2 31.9 %collective-permute-start.1 = (bf16[128,1536]{1,0:T(8,128)(2,1)S(1)}, bf16[128,1536]{1,0:T(8,128)(2,1)S(1)}, u32[]{:S(2)}, u32[]{:S(2)}) collective-permute-start(bf16[128,1536]{1,0:T(8,128)(2,1)S(1)} %slice.8.refs_0_), channel_id=1, source_target_pairs={{0,2},{1,3},{2,4},{3,5},{4,6},{5,7},{6,0},{7,1},{8,10},{9,11},{10,... | collective-permute-start | bytes 1179656 | tf_op jit(solution)/shard_map/ppermute | solution.py:21
  43.2 17.5 %copy-start.1 = (bf16[128,1536]{1,0:T(8,128)(2,1)}, bf16[128,1536]{1,0:T(8,128)(2,1)S(1)}, u32[]{:S(2)}) copy-start(bf16[128,1536]{1,0:T(8,128)(2,1)S(1)} %collective-permute-done.refs_1_) | copy-start | bytes 1179652
  43.2 9.0 %collective-permute-start.4 = (bf16[128,1536]{1,0:T(8,128)(2,1)S(1)}, bf16[128,1536]{1,0:T(8,128)(2,1)S(1)}, u32[]{:S(2)}, u32[]{:S(2)}) collective-permute-start(bf16[128,1536]{1,0:T(8,128)(2,1)S(1)} %collective-permute-done.refs_1_), channel_id=1, source_target_pairs={{0,6},{1,7},{2,0},{3,1},{4,2},{5,3},{6,4},{7,5},{8,14},{9,15},{10,... | collective-permute-start | bytes 1179656 | tf_op jit(solution)/shard_map/ppermute | solution.py:21
  45.7 15.0 %collective-permute-start.3 = (bf16[128,1536]{1,0:T(8,128)(2,1)S(1)}, bf16[128,1536]{1,0:T(8,128)(2,1)S(1)}, u32[]{:S(2)}, u32[]{:S(2)}) collective-permute-start(bf16[128,1536]{1,0:T(8,128)(2,1)S(1)} %slice.8.refs_0_), channel_id=1, source_target_pairs={{0,6},{1,7},{2,0},{3,1},{4,2},{5,3},{6,4},{7,5},{8,14},{9,15},{10,... | collective-permute-start | bytes 1179656 | tf_op jit(solution)/shard_map/ppermute | solution.py:21
  46.2 14.5 %collective-permute-start.2 = (bf16[128,1536]{1,0:T(8,128)(2,1)S(1)}, bf16[128,1536]{1,0:T(8,128)(2,1)S(1)}, u32[]{:S(2)}, u32[]{:S(2)}) collective-permute-start(bf16[128,1536]{1,0:T(8,128)(2,1)S(1)} %collective-permute-done.refs_1_), channel_id=1, source_target_pairs={{0,2},{1,3},{2,4},{3,5},{4,6},{5,7},{6,0},{7,1},{8,10},{9,11},{10,... | collective-permute-start | bytes 1179656 | tf_op jit(solution)/shard_map/ppermute | solution.py:21
  47.1 13.6 %copy-start.2 = (bf16[128,1536]{1,0:T(8,128)(2,1)}, bf16[128,1536]{1,0:T(8,128)(2,1)S(1)}, u32[]{:S(2)}) copy-start(bf16[128,1536]{1,0:T(8,128)(2,1)S(1)} %collective-permute-done.1.refs_2_) | copy-start | bytes 1179652
  47.1 16.9 %collective-permute-start.5 = (bf16[128,1536]{1,0:T(8,128)(2,1)S(1)}, bf16[128,1536]{1,0:T(8,128)(2,1)S(1)}, u32[]{:S(2)}, u32[]{:S(2)}) collective-permute-start(bf16[128,1536]{1,0:T(8,128)(2,1)S(1)} %collective-permute-done.1.refs_2_), channel_id=1, source_target_pairs={{0,2},{1,3},{2,4},{3,5},{4,6},{5,7},{6,0},{7,1},{8,10},{9,11},{10,... | collective-permute-start | bytes 1179656 | tf_op jit(solution)/shard_map/ppermute | solution.py:21
  52.3 11.8 %copy-start.3 = (bf16[128,1536]{1,0:T(8,128)(2,1)}, bf16[128,1536]{1,0:T(8,128)(2,1)S(1)}, u32[]{:S(2)}) copy-start(bf16[128,1536]{1,0:T(8,128)(2,1)S(1)} %collective-permute-done.4.refs_5_) | copy-start | bytes 1179652
  52.3 16.9 %collective-permute-start.6 = (bf16[128,1536]{1,0:T(8,128)(2,1)S(1)}, bf16[128,1536]{1,0:T(8,128)(2,1)}, u32[]{:S(2)}, u32[]{:S(2)}) collective-permute-start(bf16[128,1536]{1,0:T(8,128)(2,1)S(1)} %collective-permute-done.4.refs_5_), channel_id=1, source_target_pairs={{0,6},{1,7},{2,0},{3,1},{4,2},{5,3},{6,4},{7,5},{8,14},{9,15},{10,... | collective-permute-start | bytes 1179656 | tf_op jit(solution)/shard_map/ppermute | solution.py:21
  60.7 3.4 %copy-start.4 = (bf16[128,1536]{1,0:T(8,128)(2,1)}, bf16[128,1536]{1,0:T(8,128)(2,1)S(1)}, u32[]{:S(2)}) copy-start(bf16[128,1536]{1,0:T(8,128)(2,1)S(1)} %collective-permute-done.3.refs_4_) | copy-start | bytes 1179652
  60.7 3.4 %copy-start.5 = (bf16[128,1536]{1,0:T(8,128)(2,1)}, bf16[128,1536]{1,0:T(8,128)(2,1)S(1)}, u32[]{:S(2)}) copy-start(bf16[128,1536]{1,0:T(8,128)(2,1)S(1)} %collective-permute-done.2.refs_3_) | copy-start | bytes 1179652
  73.6 5.8 %collective-permute-start.7 = (bf16[448,1536]{1,0:T(8,128)(2,1)}, bf16[448,1536]{1,0:T(8,128)(2,1)}, u32[]{:S(2)}, u32[]{:S(2)}) collective-permute-start(bf16[448,1536]{1,0:T(8,128)(2,1)} %send_part.2), channel_id=1, source_target_pairs={{0,1},{1,0},{2,3},{3,2},{4,5},{5,4},{6,7},{7,6},{8,9},{9,8},{10,11... | collective-permute-start | bytes 4128776 | tf_op jit(solution)/shard_map/ppermute | solution.py:21
  130.5 85.7 %all-to-all-start.2 = ((bf16[16,336,128]{2,1,0:T(8,128)(2,1)}), bf16[16,336,128]{2,1,0:T(8,128)(2,1)}, u32[]{:S(2)}, u32[]{:S(2)}) async-start(bf16[16,336,128]{2,1,0:T(8,128)(2,1)} %trim.1), calls=%async_computation.2 | async-start | bytes 2752512 | tf_op jit(solution)/shard_map/all_to_all | solution.py:301
  137.1 11.3 %copy-start.7 = (bf16[128,512]{1,0:T(8,128)(2,1)}, bf16[128,512]{1,0:T(8,128)(2,1)S(1)}, u32[]{:S(2)}) copy-start(bf16[128,512]{1,0:T(8,128)(2,1)S(1)} %slice.9.refs_0_) | copy-start | bytes 393220
  137.1 7.8 %collective-permute-start.8 = (bf16[128,512]{1,0:T(8,128)(2,1)S(1)}, bf16[128,512]{1,0:T(8,128)(2,1)S(1)}, u32[]{:S(2)}, u32[]{:S(2)}) collective-permute-start(bf16[128,512]{1,0:T(8,128)(2,1)S(1)} %slice.9.refs_0_), channel_id=1, source_target_pairs={{0,8},{1,9},{2,10},{3,11},{4,12},{5,13},{6,14},{7,15},{8,0},{9,1},... | collective-permute-start | bytes 393224 | tf_op jit(solution)/shard_map/ppermute | solution.py:21
  137.8 12.1 %collective-permute-start.9 = (bf16[128,512]{1,0:T(8,128)(2,1)S(1)}, bf16[128,512]{1,0:T(8,128)(2,1)S(1)}, u32[]{:S(2)}, u32[]{:S(2)}) collective-permute-start(bf16[128,512]{1,0:T(8,128)(2,1)S(1)} %slice.9.refs_0_), channel_id=1, source_target_pairs={{0,2},{1,3},{2,4},{3,5},{4,6},{5,7},{6,0},{7,1},{8,10},{9,11},{10,... | collective-permute-start | bytes 393224 | tf_op jit(solution)/shard_map/ppermute | solution.py:21
  144.9 8.8 %copy-start.8 = (bf16[128,512]{1,0:T(8,128)(2,1)}, bf16[128,512]{1,0:T(8,128)(2,1)S(1)}, u32[]{:S(2)}) copy-start(bf16[128,512]{1,0:T(8,128)(2,1)S(1)} %collective-permute-done.8.refs_1_) | copy-start | bytes 393220
  144.9 5.5 %collective-permute-start.12 = (bf16[128,512]{1,0:T(8,128)(2,1)S(1)}, bf16[128,512]{1,0:T(8,128)(2,1)S(1)}, u32[]{:S(2)}, u32[]{:S(2)}) collective-permute-start(bf16[128,512]{1,0:T(8,128)(2,1)S(1)} %collective-permute-done.8.refs_1_), channel_id=1, source_target_pairs={{0,6},{1,7},{2,0},{3,1},{4,2},{5,3},{6,4},{7,5},{8,14},{9,15},{10,... | collective-permute-start | bytes 393224 | tf_op jit(solution)/shard_map/ppermute | solution.py:21
  148.4 5.3 %collective-permute-start.11 = (bf16[128,512]{1,0:T(8,128)(2,1)S(1)}, bf16[128,512]{1,0:T(8,128)(2,1)S(1)}, u32[]{:S(2)}, u32[]{:S(2)}) collective-permute-start(bf16[128,512]{1,0:T(8,128)(2,1)S(1)} %slice.9.refs_0_), channel_id=1, source_target_pairs={{0,6},{1,7},{2,0},{3,1},{4,2},{5,3},{6,4},{7,5},{8,14},{9,15},{10,... | collective-permute-start | bytes 393224 | tf_op jit(solution)/shard_map/ppermute | solution.py:21
  148.5 5.4 %collective-permute-start.10 = (bf16[128,512]{1,0:T(8,128)(2,1)S(1)}, bf16[128,512]{1,0:T(8,128)(2,1)S(1)}, u32[]{:S(2)}, u32[]{:S(2)}) collective-permute-start(bf16[128,512]{1,0:T(8,128)(2,1)S(1)} %collective-permute-done.8.refs_1_), channel_id=1, source_target_pairs={{0,2},{1,3},{2,4},{3,5},{4,6},{5,7},{6,0},{7,1},{8,10},{9,11},{10,... | collective-permute-start | bytes 393224 | tf_op jit(solution)/shard_map/ppermute | solution.py:21
  149.9 4.0 %copy-start.9 = (bf16[128,512]{1,0:T(8,128)(2,1)}, bf16[128,512]{1,0:T(8,128)(2,1)S(1)}, u32[]{:S(2)}) copy-start(bf16[128,512]{1,0:T(8,128)(2,1)S(1)} %collective-permute-done.9.refs_2_) | copy-start | bytes 393220
  149.9 5.4 %collective-permute-start.13 = (bf16[128,512]{1,0:T(8,128)(2,1)S(1)}, bf16[128,512]{1,0:T(8,128)(2,1)S(1)}, u32[]{:S(2)}, u32[]{:S(2)}) collective-permute-start(bf16[128,512]{1,0:T(8,128)(2,1)S(1)} %collective-permute-done.9.refs_2_), channel_id=1, source_target_pairs={{0,2},{1,3},{2,4},{3,5},{4,6},{5,7},{6,0},{7,1},{8,10},{9,11},{10,... | collective-permute-start | bytes 393224 | tf_op jit(solution)/shard_map/ppermute | solution.py:21
  150.4 5.0 %copy-start.10 = (bf16[128,512]{1,0:T(8,128)(2,1)}, bf16[128,512]{1,0:T(8,128)(2,1)S(1)}, u32[]{:S(2)}) copy-start(bf16[128,512]{1,0:T(8,128)(2,1)S(1)} %collective-permute-done.12.refs_5_) | copy-start | bytes 393220
  150.4 5.8 %collective-permute-start.14 = (bf16[128,512]{1,0:T(8,128)(2,1)S(1)}, bf16[128,512]{1,0:T(8,128)(2,1)}, u32[]{:S(2)}, u32[]{:S(2)}) collective-permute-start(bf16[128,512]{1,0:T(8,128)(2,1)S(1)} %collective-permute-done.12.refs_5_), channel_id=1, source_target_pairs={{0,6},{1,7},{2,0},{3,1},{4,2},{5,3},{6,4},{7,5},{8,14},{9,15},{10,... | collective-permute-start | bytes 393224 | tf_op jit(solution)/shard_map/ppermute | solution.py:21
  153.7 1.6 copy-start.11
  159.2 5.8 %collective-permute-start.15 = (bf16[448,512]{1,0:T(8,128)(2,1)}, bf16[448,512]{1,0:T(8,128)(2,1)}, u32[]{:S(2)}, u32[]{:S(2)}) collective-permute-start(bf16[448,512]{1,0:T(8,128)(2,1)} %send_part.3), channel_id=1, source_target_pairs={{0,1},{1,0},{2,3},{3,2},{4,5},{5,4},{6,7},{7,6},{8,9},{9,8},{10,11... | collective-permute-start | bytes 1376264 | tf_op jit(solution)/shard_map/ppermute | solution.py:21
  168.6 11.0 %collective-permute-start.16 = (bf16[224,128]{1,0:T(8,128)(2,1)}, bf16[224,128]{1,0:T(8,128)(2,1)S(1)}, u32[]{:S(2)}, u32[]{:S(2)}) collective-permute-start(bf16[224,128]{1,0:T(8,128)(2,1)} %get-tuple-element.23), channel_id=1, source_target_pairs={{0,16},{16,32},{32,48},{48,64},{64,80},{80,96},{96,112},{112,0},{1... | collective-permute-start | bytes 172040 | tf_op jit(solution)/shard_map/ppermute | solution.py:296
  169.5 13.5 %collective-permute-start.17 = (bf16[224,128]{1,0:T(8,128)(2,1)}, bf16[224,128]{1,0:T(8,128)(2,1)S(1)}, u32[]{:S(2)}, u32[]{:S(2)}) collective-permute-start(bf16[224,128]{1,0:T(8,128)(2,1)} %get-tuple-element.24), channel_id=1, source_target_pairs={{0,32},{16,48},{32,64},{48,80},{64,96},{80,112},{96,0},{112,16},{1... | collective-permute-start | bytes 172040 | tf_op jit(solution)/shard_map/ppermute | solution.py:296
  173.9 10.5 %collective-permute-start.18 = (bf16[224,128]{1,0:T(8,128)(2,1)}, bf16[224,128]{1,0:T(8,128)(2,1)S(1)}, u32[]{:S(2)}, u32[]{:S(2)}) collective-permute-start(bf16[224,128]{1,0:T(8,128)(2,1)} %get-tuple-element.25), channel_id=1, source_target_pairs={{0,48},{16,64},{32,80},{48,96},{64,112},{80,0},{96,16},{112,32},{1... | collective-permute-start | bytes 172040 | tf_op jit(solution)/shard_map/ppermute | solution.py:296
  175.1 10.7 %collective-permute-start.19 = (bf16[224,128]{1,0:T(8,128)(2,1)}, bf16[224,128]{1,0:T(8,128)(2,1)S(1)}, u32[]{:S(2)}, u32[]{:S(2)}) collective-permute-start(bf16[224,128]{1,0:T(8,128)(2,1)} %get-tuple-element.26), channel_id=1, source_target_pairs={{0,64},{16,80},{32,96},{48,112},{64,0},{80,16},{96,32},{112,48},{1... | collective-permute-start | bytes 172040 | tf_op jit(solution)/shard_map/ppermute | solution.py:296
  179.4 7.6 %collective-permute-start.20 = (bf16[224,128]{1,0:T(8,128)(2,1)}, bf16[224,128]{1,0:T(8,128)(2,1)S(1)}, u32[]{:S(2)}, u32[]{:S(2)}) collective-permute-start(bf16[224,128]{1,0:T(8,128)(2,1)} %get-tuple-element.27), channel_id=1, source_target_pairs={{0,80},{16,96},{32,112},{48,0},{64,16},{80,32},{96,48},{112,64},{1... | collective-permute-start | bytes 172040 | tf_op jit(solution)/shard_map/ppermute | solution.py:296
  179.6 6.2 %copy-start.15 = (bf16[224,128]{1,0:T(8,128)(2,1)}, bf16[224,128]{1,0:T(8,128)(2,1)S(1)}, u32[]{:S(2)}) copy-start(bf16[224,128]{1,0:T(8,128)(2,1)S(1)} %collective-permute-done.16.refs_1_) | copy-start | bytes 172036
  179.6 10.4 %collective-permute-start.21 = (bf16[224,128]{1,0:T(8,128)(2,1)}, bf16[224,128]{1,0:T(8,128)(2,1)S(1)}, u32[]{:S(2)}, u32[]{:S(2)}) collective-permute-start(bf16[224,128]{1,0:T(8,128)(2,1)} %get-tuple-element.28), channel_id=1, source_target_pairs={{0,96},{16,112},{32,0},{48,16},{64,32},{80,48},{96,64},{112,80},{1... | collective-permute-start | bytes 172040 | tf_op jit(solution)/shard_map/ppermute | solution.py:296
  183.0 10.4 %copy-start.16 = (bf16[224,128]{1,0:T(8,128)(2,1)}, bf16[224,128]{1,0:T(8,128)(2,1)S(1)}, u32[]{:S(2)}) copy-start(bf16[224,128]{1,0:T(8,128)(2,1)S(1)} %collective-permute-done.17.refs_2_) | copy-start | bytes 172036
  183.0 8.9 %collective-permute-start.22 = (bf16[224,128]{1,0:T(8,128)(2,1)}, bf16[224,128]{1,0:T(8,128)(2,1)S(1)}, u32[]{:S(2)}, u32[]{:S(2)}) collective-permute-start(bf16[224,128]{1,0:T(8,128)(2,1)} %get-tuple-element.29), channel_id=1, source_target_pairs={{0,112},{16,0},{32,16},{48,32},{64,48},{80,64},{96,80},{112,96},{1... | collective-permute-start | bytes 172040 | tf_op jit(solution)/shard_map/ppermute | solution.py:296
  184.4 9.2 %copy-start.17 = (bf16[224,128]{1,0:T(8,128)(2,1)}, bf16[224,128]{1,0:T(8,128)(2,1)S(1)}, u32[]{:S(2)}) copy-start(bf16[224,128]{1,0:T(8,128)(2,1)S(1)} %collective-permute-done.18.refs_3_) | copy-start | bytes 172036
  184.4 7.6 %collective-permute-start.23 = (bf16[224,128]{1,0:T(8,128)(2,1)}, bf16[224,128]{1,0:T(8,128)(2,1)S(1)}, u32[]{:S(2)}, u32[]{:S(2)}) collective-permute-start(bf16[224,128]{1,0:T(8,128)(2,1)} %get-tuple-element.22.refs_0_), channel_id=1, source_target_pairs={{0,128},{16,144},{32,160},{48,176},{64,192},{80,208},{96,224},{112... | collective-permute-start | bytes 172040 | tf_op jit(solution)/shard_map/ppermute | solution.py:337
  185.8 9.4 %copy-start.18 = (bf16[224,128]{1,0:T(8,128)(2,1)}, bf16[224,128]{1,0:T(8,128)(2,1)S(1)}, u32[]{:S(2)}) copy-start(bf16[224,128]{1,0:T(8,128)(2,1)S(1)} %collective-permute-done.19.refs_4_) | copy-start | bytes 172036
  185.9 7.5 %collective-permute-start.24 = (bf16[224,128]{1,0:T(8,128)(2,1)S(1)}, bf16[224,128]{1,0:T(8,128)(2,1)S(1)}, u32[]{:S(2)}, u32[]{:S(2)}) collective-permute-start(bf16[224,128]{1,0:T(8,128)(2,1)S(1)} %collective-permute-done.16.refs_1_), channel_id=1, source_target_pairs={{0,128},{16,144},{32,160},{48,176},{64,192},{80,208},{96,224},{112... | collective-permute-start | bytes 172040 | tf_op jit(solution)/shard_map/ppermute | solution.py:337
  187.0 8.2 %copy-start.19 = (bf16[224,128]{1,0:T(8,128)(2,1)}, bf16[224,128]{1,0:T(8,128)(2,1)S(1)}, u32[]{:S(2)}) copy-start(bf16[224,128]{1,0:T(8,128)(2,1)S(1)} %collective-permute-done.20.refs_5_) | copy-start | bytes 172036
  187.0 6.5 %collective-permute-start.25 = (bf16[224,128]{1,0:T(8,128)(2,1)S(1)}, bf16[224,128]{1,0:T(8,128)(2,1)S(1)}, u32[]{:S(2)}, u32[]{:S(2)}) collective-permute-start(bf16[224,128]{1,0:T(8,128)(2,1)S(1)} %collective-permute-done.17.refs_2_), channel_id=1, source_target_pairs={{0,128},{16,144},{32,160},{48,176},{64,192},{80,208},{96,224},{112... | collective-permute-start | bytes 172040 | tf_op jit(solution)/shard_map/ppermute | solution.py:337
  190.1 5.9 %copy-start.20 = (bf16[224,128]{1,0:T(8,128)(2,1)}, bf16[224,128]{1,0:T(8,128)(2,1)S(1)}, u32[]{:S(2)}) copy-start(bf16[224,128]{1,0:T(8,128)(2,1)S(1)} %collective-permute-done.21.refs_6_) | copy-start | bytes 172036
  190.1 5.2 %collective-permute-start.26 = (bf16[224,128]{1,0:T(8,128)(2,1)S(1)}, bf16[224,128]{1,0:T(8,128)(2,1)S(1)}, u32[]{:S(2)}, u32[]{:S(2)}) collective-permute-start(bf16[224,128]{1,0:T(8,128)(2,1)S(1)} %collective-permute-done.18.refs_3_), channel_id=1, source_target_pairs={{0,128},{16,144},{32,160},{48,176},{64,192},{80,208},{96,224},{112... | collective-permute-start | bytes 172040 | tf_op jit(solution)/shard_map/ppermute | solution.py:337
  191.9 5.5 %copy-start.21 = (bf16[224,128]{1,0:T(8,128)(2,1)}, bf16[224,128]{1,0:T(8,128)(2,1)S(1)}, u32[]{:S(2)}) copy-start(bf16[224,128]{1,0:T(8,128)(2,1)S(1)} %collective-permute-done.22.refs_7_) | copy-start | bytes 172036
  191.9 3.4 %collective-permute-start.27 = (bf16[224,128]{1,0:T(8,128)(2,1)S(1)}, bf16[224,128]{1,0:T(8,128)(2,1)S(1)}, u32[]{:S(2)}, u32[]{:S(2)}) collective-permute-start(bf16[224,128]{1,0:T(8,128)(2,1)S(1)} %collective-permute-done.19.refs_4_), channel_id=1, source_target_pairs={{0,128},{16,144},{32,160},{48,176},{64,192},{80,208},{96,224},{112... | collective-permute-start | bytes 172040 | tf_op jit(solution)/shard_map/ppermute | solution.py:337
  192.0 5.4 %copy-start.22 = (bf16[224,128]{1,0:T(8,128)(2,1)}, bf16[224,128]{1,0:T(8,128)(2,1)S(1)}, u32[]{:S(2)}) copy-start(bf16[224,128]{1,0:T(8,128)(2,1)S(1)} %collective-permute-done.23.refs_8_) | copy-start | bytes 172036
  192.0 4.0 %collective-permute-start.28 = (bf16[224,128]{1,0:T(8,128)(2,1)S(1)}, bf16[224,128]{1,0:T(8,128)(2,1)S(1)}, u32[]{:S(2)}, u32[]{:S(2)}) collective-permute-start(bf16[224,128]{1,0:T(8,128)(2,1)S(1)} %collective-permute-done.20.refs_5_), channel_id=1, source_target_pairs={{0,128},{16,144},{32,160},{48,176},{64,192},{80,208},{96,224},{112... | collective-permute-start | bytes 172040 | tf_op jit(solution)/shard_map/ppermute | solution.py:337
  193.4 4.0 %copy-start.23 = (bf16[224,128]{1,0:T(8,128)(2,1)}, bf16[224,128]{1,0:T(8,128)(2,1)S(1)}, u32[]{:S(2)}) copy-start(bf16[224,128]{1,0:T(8,128)(2,1)S(1)} %collective-permute-done.24.refs_9_) | copy-start | bytes 172036
  193.4 4.0 %collective-permute-start.29 = (bf16[224,128]{1,0:T(8,128)(2,1)S(1)}, bf16[224,128]{1,0:T(8,128)(2,1)S(1)}, u32[]{:S(2)}, u32[]{:S(2)}) collective-permute-start(bf16[224,128]{1,0:T(8,128)(2,1)S(1)} %collective-permute-done.21.refs_6_), channel_id=1, source_target_pairs={{0,128},{16,144},{32,160},{48,176},{64,192},{80,208},{96,224},{112... | collective-permute-start | bytes 172040 | tf_op jit(solution)/shard_map/ppermute | solution.py:337
  193.6 3.8 %copy-start.24 = (bf16[224,128]{1,0:T(8,128)(2,1)}, bf16[224,128]{1,0:T(8,128)(2,1)S(1)}, u32[]{:S(2)}) copy-start(bf16[224,128]{1,0:T(8,128)(2,1)S(1)} %collective-permute-done.25.refs_10_) | copy-start | bytes 172036
  193.6 5.0 %collective-permute-start.30 = (bf16[224,128]{1,0:T(8,128)(2,1)S(1)}, bf16[224,128]{1,0:T(8,128)(2,1)}, u32[]{:S(2)}, u32[]{:S(2)}) collective-permute-start(bf16[224,128]{1,0:T(8,128)(2,1)S(1)} %collective-permute-done.22.refs_7_), channel_id=1, source_target_pairs={{0,128},{16,144},{32,160},{48,176},{64,192},{80,208},{96,224},{112... | collective-permute-start | bytes 172040 | tf_op jit(solution)/shard_map/ppermute | solution.py:337
  195.2 2.2 copy-start.25
  195.2 2.2 copy-start.26
  201.3 9.9 %collective-permute-start.31 = (bf16[224,128]{1,0:T(8,128)(2,1)}, bf16[224,128]{1,0:T(8,128)(2,1)}, u32[]{:S(2)}, u32[]{:S(2)}) collective-permute-start(bf16[224,128]{1,0:T(8,128)(2,1)} %get-tuple-element.31), channel_id=1, source_target_pairs={{0,16},{16,32},{32,48},{48,64},{64,80},{80,96},{96,112},{112,0},{1... | collective-permute-start | bytes 172040 | tf_op jit(solution)/shard_map/ppermute | solution.py:296
  202.5 10.6 %collective-permute-start.32 = (bf16[224,128]{1,0:T(8,128)(2,1)}, bf16[224,128]{1,0:T(8,128)(2,1)}, u32[]{:S(2)}, u32[]{:S(2)}) collective-permute-start(bf16[224,128]{1,0:T(8,128)(2,1)} %get-tuple-element.32), channel_id=1, source_target_pairs={{0,32},{16,48},{32,64},{48,80},{64,96},{80,112},{96,0},{112,16},{1... | collective-permute-start | bytes 172040 | tf_op jit(solution)/shard_map/ppermute | solution.py:296
  202.6 16.1 %collective-permute-start.33 = (bf16[224,128]{1,0:T(8,128)(2,1)}, bf16[224,128]{1,0:T(8,128)(2,1)}, u32[]{:S(2)}, u32[]{:S(2)}) collective-permute-start(bf16[224,128]{1,0:T(8,128)(2,1)} %get-tuple-element.33), channel_id=1, source_target_pairs={{0,48},{16,64},{32,80},{48,96},{64,112},{80,0},{96,16},{112,32},{1... | collective-permute-start | bytes 172040 | tf_op jit(solution)/shard_map/ppermute | solution.py:296
  205.8 12.9 %collective-permute-start.34 = (bf16[224,128]{1,0:T(8,128)(2,1)}, bf16[224,128]{1,0:T(8,128)(2,1)}, u32[]{:S(2)}, u32[]{:S(2)}) collective-permute-start(bf16[224,128]{1,0:T(8,128)(2,1)} %get-tuple-element.34), channel_id=1, source_target_pairs={{0,64},{16,80},{32,96},{48,112},{64,0},{80,16},{96,32},{112,48},{1... | collective-permute-start | bytes 172040 | tf_op jit(solution)/shard_map/ppermute | solution.py:296
  208.0 10.7 %collective-permute-start.35 = (bf16[224,128]{1,0:T(8,128)(2,1)}, bf16[224,128]{1,0:T(8,128)(2,1)}, u32[]{:S(2)}, u32[]{:S(2)}) collective-permute-start(bf16[224,128]{1,0:T(8,128)(2,1)} %get-tuple-element.35), channel_id=1, source_target_pairs={{0,80},{16,96},{32,112},{48,0},{64,16},{80,32},{96,48},{112,64},{1... | collective-permute-start | bytes 172040 | tf_op jit(solution)/shard_map/ppermute | solution.py:296
  211.2 8.0 %collective-permute-start.36 = (bf16[224,128]{1,0:T(8,128)(2,1)}, bf16[224,128]{1,0:T(8,128)(2,1)}, u32[]{:S(2)}, u32[]{:S(2)}) collective-permute-start(bf16[224,128]{1,0:T(8,128)(2,1)} %get-tuple-element.36), channel_id=1, source_target_pairs={{0,96},{16,112},{32,0},{48,16},{64,32},{80,48},{96,64},{112,80},{1... | collective-permute-start | bytes 172040 | tf_op jit(solution)/shard_map/ppermute | solution.py:296
  213.2 6.8 %collective-permute-start.37 = (bf16[224,128]{1,0:T(8,128)(2,1)}, bf16[224,128]{1,0:T(8,128)(2,1)}, u32[]{:S(2)}, u32[]{:S(2)}) collective-permute-start(bf16[224,128]{1,0:T(8,128)(2,1)} %get-tuple-element.37), channel_id=1, source_target_pairs={{0,112},{16,0},{32,16},{48,32},{64,48},{80,64},{96,80},{112,96},{1... | collective-permute-start | bytes 172040 | tf_op jit(solution)/shard_map/ppermute | solution.py:296
  (5 other events, 4.8 us)

commit v3 on v2

--- a/solution.py
+++ b/solution.py
@@ -58,22 +58,22 @@
         out[:, lane : lane + 256] = token_product(acts, grads, lane, 256).astype(out.dtype)
 
 
-def column_tile(rows, cols):
-    return pl.BlockSpec((rows, cols), lambda i: (0, i))
-
-
-def send_part(acts, grads):
+def column_tile(rows, cols, spot=0):
+    return pl.BlockSpec((rows, cols), lambda i: (0, spot + i))
+
+
+def send_part(acts, mine, grads, first):
     tokens, cols = grads[0].shape
     rows, tile = acts.shape[1] // 2, cols // SEND_STEPS
     return pl.pallas_call(
         send_kernel,
         grid=(SEND_STEPS,),
-        in_specs=[half_acts(acts, 1)] + [column_tile(tokens, tile)] * 8,
+        in_specs=[half_acts(acts, 1), column_tile(tokens, tile, first // tile)] + [column_tile(tokens, tile)] * 7,
         out_specs=column_tile(rows, tile),
         out_shape=jax.ShapeDtypeStruct((rows, cols), jnp.bfloat16),
         compiler_params=WIDE,
         name="send_part",
-    )(acts, *grads)
+    )(acts, mine, *grads)
 
 
 def split_rows(block, rows, per_slot):
@@ -92,8 +92,9 @@
         out[...] = slots[(z + offset) & 7]
 
 
-def step_kernel(acts, *refs):
-    grads, (other, weights, moment, new_moment), rest = refs[:8], refs[8:12], refs[12:]
+def step_kernel(carried, acts, *refs):
+    grads, (other, weights, moment), rest = refs[:8], refs[8:11], refs[11 + carried :]
+    new_moment, rest = rest[0], rest[1:]
     half = rest[-1]
     rows, cols = other.shape
     for lane in range(0, cols, 256):
@@ -109,14 +110,13 @@
         spread(half, rest[:-1])
 
 
-def step(acts, grads, other, weights, moment, first, apart):
+def step(acts, mine, grads, other, weights, moment, first, new_moment, apart):
     rows, cols = other.shape
     steps = 1 if apart else STEP_STEPS
     tile = cols // steps
-    if first % tile:
-        weights, moment, first = weights[:, first : first + cols], moment[:, first : first + cols], 0
     columns = pl.BlockSpec((rows, tile), lambda i: (0, first // tile + i))
-    moved = jax.ShapeDtypeStruct((rows, cols), jnp.bfloat16)
+    moved = jax.ShapeDtypeStruct(weights.shape, jnp.bfloat16)
+    carried = [] if new_moment is None else [new_moment]
     if apart:
         part = jax.ShapeDtypeStruct((rows * cols // LANES // 8, LANES), jnp.bfloat16)
         outs, specs = [part] * 8, [pl.BlockSpec(part.shape, lambda i: (0, 0))] * 8
@@ -126,17 +126,19 @@
         specs = [pl.BlockSpec((tile // LANES, rows, LANES), lambda i: (i, 0, 0))]
         scratch = []
     new_moment, *half = pl.pallas_call(
-        step_kernel,
+        functools.partial(step_kernel, len(carried)),
         grid=(steps,),
-        in_specs=[half_acts(acts, 0)]
-        + [column_tile(grads[0].shape[0], tile)] * 8
-        + [column_tile(rows, tile), columns, columns],
-        out_specs=[column_tile(rows, tile)] + specs,
+        in_specs=[half_acts(acts, 0), column_tile(mine.shape[0], tile, first // tile)]
+        + [column_tile(mine.shape[0], tile)] * 7
+        + [column_tile(rows, tile), columns, columns]
+        + [pl.BlockSpec(memory_space=pl.ANY)] * len(carried),
+        out_specs=[columns] + specs,
         out_shape=[moved] + outs,
         scratch_shapes=scratch,
+        input_output_aliases={12: 0} if carried else {},
         compiler_params=WIDE,
         name="step",
-    )(acts, *grads, other, weights, moment)
+    )(acts, mine, *grads, other, weights, moment, *carried)
     return new_moment, half if apart else half[0].reshape(NODES, -1, LANES)
 
 
@@ -179,7 +181,7 @@
 
 
 def trim(halves):
-    tile = halves.shape[1] if halves.shape[1] % 112 else 112
+    tile = halves.shape[1] // 2
     spec = pl.BlockSpec((NODES, tile, LANES), lambda i: (0, i, 0))
     return pl.pallas_call(
         trim_kernel,
@@ -226,7 +228,6 @@
         out_specs=[spec] * 8,
         out_shape=[out] * 8,
         scratch_shapes=[pltpu.VMEM((8, tile, LANES), jnp.bfloat16)] * 3,
-        compiler_params=WIDE,
         name="trim_apart",
     )(*near, *far)
 
@@ -286,12 +287,9 @@
     )(laid, *pieces)
 
 
-ORDER = (4, 5, 3, 6, 2, 7, 1)
-
-
 def ring_exchange(pieces):
     got = {0: pieces[0]}
-    for offset in ORDER:
+    for offset in range(1, 8):
         pairs = [(n, (n & 8) | ((n + offset) & 7)) for n in range(NODES)]
         got[offset] = lax.ppermute(pieces[offset], "node", pairs)
     return [got[offset] for offset in range(8)]
@@ -316,14 +314,13 @@
         below_far, above_far = shard_move(far, up_y), shard_move(far, down_y)
         opposite_own = shard_move(below_own, up_y)
         opposite_far = shard_move(above_far, down_y)
-        pieces.append([own, far, below_own, below_far, above_own, above_far, opposite_own, opposite_far])
-
-    moments, halves = [], []
+        pieces.append([far, below_own, below_far, above_own, above_far, opposite_own, opposite_far])
+
+    new_moment, halves = None, []
     for k, cut in enumerate(cuts):
-        sent = send_part(acts, pieces[k])
+        sent = send_part(acts, grads, pieces[k], cut.start)
         other = shard_move(sent, other_core)
-        new_moment, half = step(acts, pieces[k], other, weights, moment, cut.start, k == 1)
-        moments.append(new_moment)
+        new_moment, half = step(acts, grads, pieces[k], other, weights, moment, cut.start, new_moment, k == 1)
         halves.append(half)
 
     exchanged = node_exchange(halves[0])
@@ -338,7 +335,6 @@
     results = trim_apart(near, far)
     arrived = ring_exchange(results)
     new_weights = lay_apart(laid, arrived, BLOCKS[0])
-    new_moment = jnp.concatenate(moments, axis=1)
     return new_weights[None], new_moment[None]
 
 

time: 225 us -> 225 us (level)
  waiting for transfers between devices: 63.9 us -> 67.9 us
  other arithmetic: 2.97 us -> 0 us
    broadcast_in_dim x1 -> x0, other arithmetic: 2.97 us -> none  [on_device(): return (new_weights[None], new_moment[None])]
    ppermute x14, waiting for transfers between devices: 3.72 us -> 6.67 us  [ring_exchange(): got[offset] = lax.ppermute(pieces[offset], 'node', pairs)]
  transfers between devices with their start and end apart: 40 -> 40, of which waited for: 18 -> 19; matrix products, arithmetic and copies ran while one was open for 2% -> 0% of each run, Pallas kernels for 5% -> 5%
where the time goes in v3:
time: 225 us; the launch traced here: 223 us
  starting transfers between devices  77.8 us (35%)
  waiting for transfers between devices  67.9 us (30%)
  blocking collectives  41.4 us (18%)
  Pallas kernels  27.5 us (12%)
  local copies, waits for them, and re-layouts  6.93 us (3%)
    ppermute x16, waiting for transfers between devices, shard_move(): return lax.ppermute(value, 'shard', [(s, target(s)) for s in range(16)])  57.5 us
    all_to_all x1, blocking collectives, node_exchange(): return lax.all_to_all(value, 'node', split_axis=0, concat_axis=0)  41.4 us
    ppermute x16, starting transfers between devices, shard_move(): return lax.ppermute(value, 'shard', [(s, target(s)) for s in range(16)])  28.6 us
    ppermute x14, starting transfers between devices, ring_exchange(): got[offset] = lax.ppermute(pieces[offset], 'node', pairs)  27.9 us
    pallas_call x2, Pallas kernels, step(): pl.pallas_call(functools.partial(step_kernel, len(carried)), grid=(steps,...  9.37 us
    ppermute x8, starting transfers between devices, on_device(): far.append(lax.ppermute(piece, 'node', [(n, n ^ 8) for n in range(NODES)]))  7.95 us
    all_to_all x1, starting transfers between devices, on_device(): lax.all_to_all(acts, 'shard', split_axis=0, concat_axis=0, axis_index_gro...  7.6 us
    pallas_call x2, Pallas kernels, send_part(): pl.pallas_call(send_kernel, grid=(SEND_STEPS,), in_specs=[half_acts(acts,...  7.56 us
  transfers between devices with their start and end apart: 40, of which 19 were waited for; matrix products, arithmetic and copies ran while one was open for 0% of the time, Pallas kernels for 5%

profile of v3, /device:TPU:1, one launch (start us, length us, event | category | flops | bytes accessed | tf_op | source)
XLA Modules:
  0.0 222.5 jit_solution(3173672175054991738)
XLA Ops:
  0.6 3.9 %copy.8 = bf16[7168,128]{1,0:T(8,128)(2,1)} copy(bf16[7168,128]{0,1:T(8,128)(2,1)} %bitcast.22) | data formatting | bytes 3670016 | tf_op jit(solution)/shard_map/transpose | solution.py:306
  4.5 7.6 %all-to-all-start = ((bf16[8,896,128]{2,1,0:T(8,128)(2,1)}), bf16[8,896,128]{2,1,0:T(8,128)(2,1)}, u32[]{:S(2)}, u32[]{:S(2)}) async-start(bf16[8,896,128]{2,1,0:T(8,128)(2,1)} %bitcast.2), calls=%async_computation | async-start | bytes 3670016 | tf_op jit(solution)/shard_map/all_to_all | solution.py:307
  12.1 3.0 %collective-permute-start = (bf16[128,1536]{1,0:T(8,128)(2,1)S(1)}, bf16[128,1536]{1,0:T(8,128)(2,1)S(1)}, u32[]{:S(2)}, u32[]{:S(2)}) collective-permute-start(bf16[128,1536]{1,0:T(8,128)(2,1)S(1)} %slice.8), channel_id=1, source_target_pairs={{0,8},{1,9},{2,10},{3,11},{4,12},{5,13},{6,14},{7,15},{8,0},{9,1},... | collective-permute-start | bytes 1179656 | tf_op jit(solution)/shard_map/ppermute | solution.py:21
  15.2 1.2 collective-permute-start.1
  16.4 26.8 %collective-permute-done.refs_1_ = bf16[128,1536]{1,0:T(8,128)(2,1)S(1)} collective-permute-done((bf16[128,1536]{1,0:T(8,128)(2,1)S(1)}, bf16[128,1536]{1,0:T(8,128)(2,1)S(1)}, u32[]{:S(2)}, u32[]{:S(2)}) %collective-permute-start) | collective-permute-done | bytes 393248 | tf_op jit(solution)/shard_map/ppermute | solution.py:21
  43.2 2.4 %collective-permute-start.4 = (bf16[128,1536]{1,0:T(8,128)(2,1)S(1)}, bf16[128,1536]{1,0:T(8,128)(2,1)S(1)}, u32[]{:S(2)}, u32[]{:S(2)}) collective-permute-start(bf16[128,1536]{1,0:T(8,128)(2,1)S(1)} %collective-permute-done.refs_1_), channel_id=1, source_target_pairs={{0,6},{1,7},{2,0},{3,1},{4,2},{5,3},{6,4},{7,5},{8,14},{9,15},{10,... | collective-permute-start | bytes 1179656 | tf_op jit(solution)/shard_map/ppermute | solution.py:21
  45.7 0.5 collective-permute-start.3
  46.2 0.9 collective-permute-start.2
  47.2 5.0 %collective-permute-done.4.refs_5_ = bf16[128,1536]{1,0:T(8,128)(2,1)S(1)} collective-permute-done((bf16[128,1536]{1,0:T(8,128)(2,1)S(1)}, bf16[128,1536]{1,0:T(8,128)(2,1)S(1)}, u32[]{:S(2)}, u32[]{:S(2)}) %collective-permute-start.4) | collective-permute-done | bytes 393248 | tf_op jit(solution)/shard_map/ppermute | solution.py:21
  52.3 3.4 %collective-permute-start.6 = (bf16[128,1536]{1,0:T(8,128)(2,1)S(1)}, bf16[128,1536]{1,0:T(8,128)(2,1)}, u32[]{:S(2)}, u32[]{:S(2)}) collective-permute-start(bf16[128,1536]{1,0:T(8,128)(2,1)S(1)} %collective-permute-done.4.refs_5_), channel_id=1, source_target_pairs={{0,6},{1,7},{2,0},{3,1},{4,2},{5,3},{6,4},{7,5},{8,14},{9,15},{10,... | collective-permute-start | bytes 1179656 | tf_op jit(solution)/shard_map/ppermute | solution.py:21
  55.7 5.0 %collective-permute-done.3.refs_4_ = bf16[128,1536]{1,0:T(8,128)(2,1)S(1)} collective-permute-done((bf16[128,1536]{1,0:T(8,128)(2,1)S(1)}, bf16[128,1536]{1,0:T(8,128)(2,1)S(1)}, u32[]{:S(2)}, u32[]{:S(2)}) %collective-permute-start.3) | collective-permute-done | bytes 393248 | tf_op jit(solution)/shard_map/ppermute | solution.py:21
  60.7 3.4 %collective-permute-done.5.refs_6_ = bf16[128,1536]{1,0:T(8,128)(2,1)S(1)} collective-permute-done((bf16[128,1536]{1,0:T(8,128)(2,1)S(1)}, bf16[128,1536]{1,0:T(8,128)(2,1)S(1)}, u32[]{:S(2)}, u32[]{:S(2)}) %collective-permute-start.5) | collective-permute-done | bytes 393248 | tf_op jit(solution)/shard_map/ppermute | solution.py:21
  64.1 0.7 copy-done.6
  64.9 4.3 %collective-permute-done.6.refs_7_ = bf16[128,1536]{1,0:T(8,128)(2,1)} collective-permute-done((bf16[128,1536]{1,0:T(8,128)(2,1)S(1)}, bf16[128,1536]{1,0:T(8,128)(2,1)}, u32[]{:S(2)}, u32[]{:S(2)}) %collective-permute-start.6) | collective-permute-done | bytes 393248 | tf_op jit(solution)/shard_map/ppermute | solution.py:21
  69.1 4.5 %send_part.2 = bf16[448,1536]{1,0:T(8,128)(2,1)} custom-call(bf16[8,896,128]{2,1,0:T(8,128)(2,1)} %all-to-all-done.acts, bf16[128,2048]{1,0:T(8,128)(2,1)} %bitcast.11, bf16[128,1536]{1,0:T(8,128)(2,1)} %copy-done.1, bf16[128,1536]{1,0:T(8,128)(2,1)} %copy-done.2, bf16[128,1536]{1,0:T(8,128)(2,1)} %copy-done.5, bf16[128,1536]{1,0:T(8,128)(2,1)} %copy-done.4, ...), custom_call_target="tpu_custom_call" | custom-call | tf_op jit(solution)/shard_map/send_part/pallas_call | solution.py:68
  73.6 2.7 %collective-permute-start.7 = (bf16[448,1536]{1,0:T(8,128)(2,1)}, bf16[448,1536]{1,0:T(8,128)(2,1)}, u32[]{:S(2)}, u32[]{:S(2)}) collective-permute-start(bf16[448,1536]{1,0:T(8,128)(2,1)} %send_part.2), channel_id=1, source_target_pairs={{0,1},{1,0},{2,3},{3,2},{4,5},{5,4},{6,7},{7,6},{8,9},{9,8},{10,11... | collective-permute-start | bytes 4128776 | tf_op jit(solution)/shard_map/ppermute | solution.py:21
  76.3 3.1 %collective-permute-done.7.refs_8_ = bf16[448,1536]{1,0:T(8,128)(2,1)} collective-permute-done((bf16[448,1536]{1,0:T(8,128)(2,1)}, bf16[448,1536]{1,0:T(8,128)(2,1)}, u32[]{:S(2)}, u32[]{:S(2)}) %collective-permute-start.7) | collective-permute-done | bytes 1376288 | tf_op jit(solution)/shard_map/ppermute | solution.py:21
  79.4 5.7 %step.2 = (bf16[448,2048]{1,0:T(8,128)(2,1)}, bf16[12,448,128]{2,1,0:T(8,128)(2,1)}) custom-call(bf16[8,896,128]{2,1,0:T(8,128)(2,1)} %all-to-all-done.acts, bf16[128,2048]{1,0:T(8,128)(2,1)} %bitcast.12, bf16[128,1536]{1,0:T(8,128)(2,1)} %copy-done.1, bf16[128,1536]{1,0:T(8,128)(2,1)} %copy-done.2, bf16[128,1536]{1,0:T(8,128)(2,1)} %copy-done.5, ...), custom_call_target="tpu_custom_call" | custom-call | tf_op jit(solution)/shard_map/step/pallas_call | solution.py:128
  85.2 41.4 %all_to_all.15.halves = bf16[16,336,128]{2,1,0:T(8,128)(2,1)} all-to-all(bf16[16,336,128]{2,1,0:T(8,128)(2,1)} %bitcast.24), channel_id=1, replica_groups=mesh['node'=16,'shard'=16] {'node'}, dimensions={0} | all-to-all | bytes 2752512 | tf_op jit(solution)/shard_map/all_to_all | solution.py:299
  126.6 3.5 %trim.1 = bf16[16,336,128]{2,1,0:T(8,128)(2,1)} custom-call(bf16[16,336,128]{2,1,0:T(8,128)(2,1)} %all_to_all.15.halves), custom_call_target="tpu_custom_call" | custom-call | tf_op jit(solution)/shard_map/trim/pallas_call | solution.py:186
  130.1 5.7 %all-to-all-start.2 = ((bf16[16,336,128]{2,1,0:T(8,128)(2,1)}), bf16[16,336,128]{2,1,0:T(8,128)(2,1)}, u32[]{:S(2)}, u32[]{:S(2)}) async-start(bf16[16,336,128]{2,1,0:T(8,128)(2,1)} %trim.1), calls=%async_computation.2 | async-start | bytes 2752512 | tf_op jit(solution)/shard_map/all_to_all | solution.py:299
  135.8 0.9 slice.9
  136.7 0.7 collective-permute-start.8
  137.4 1.0 collective-permute-start.9
  138.5 6.0 %collective-permute-done.8.refs_1_ = bf16[128,512]{1,0:T(8,128)(2,1)S(1)} collective-permute-done((bf16[128,512]{1,0:T(8,128)(2,1)S(1)}, bf16[128,512]{1,0:T(8,128)(2,1)S(1)}, u32[]{:S(2)}, u32[]{:S(2)}) %collective-permute-start.8) | collective-permute-done | bytes 131104 | tf_op jit(solution)/shard_map/ppermute | solution.py:21
  144.5 3.5 %collective-permute-start.12 = (bf16[128,512]{1,0:T(8,128)(2,1)S(1)}, bf16[128,512]{1,0:T(8,128)(2,1)S(1)}, u32[]{:S(2)}, u32[]{:S(2)}) collective-permute-start(bf16[128,512]{1,0:T(8,128)(2,1)S(1)} %collective-permute-done.8.refs_1_), channel_id=1, source_target_pairs={{0,6},{1,7},{2,0},{3,1},{4,2},{5,3},{6,4},{7,5},{8,14},{9,15},{10,... | collective-permute-start | bytes 393224 | tf_op jit(solution)/shard_map/ppermute | solution.py:21
  148.0 1.4 collective-permute-start.10
  149.5 0.3 collective-permute-start.13
  150.0 3.3 %collective-permute-start.14 = (bf16[128,512]{1,0:T(8,128)(2,1)S(1)}, bf16[128,512]{1,0:T(8,128)(2,1)}, u32[]{:S(2)}, u32[]{:S(2)}) collective-permute-start(bf16[128,512]{1,0:T(8,128)(2,1)S(1)} %collective-permute-done.12.refs_5_), channel_id=1, source_target_pairs={{0,6},{1,7},{2,0},{3,1},{4,2},{5,3},{6,4},{7,5},{8,14},{9,15},{10,... | collective-permute-start | bytes 393224 | tf_op jit(solution)/shard_map/ppermute | solution.py:21
  153.5 1.4 collective-permute-done.13.refs_6_
  154.9 0.6 copy-done.12
  155.8 3.1 %send_part.3 = bf16[448,512]{1,0:T(8,128)(2,1)} custom-call(bf16[8,896,128]{2,1,0:T(8,128)(2,1)} %all-to-all-done.acts, bf16[128,2048]{1,0:T(8,128)(2,1)} %bitcast.14, bf16[128,512]{1,0:T(8,128)(2,1)} %copy-done.7, bf16[128,512]{1,0:T(8,128)(2,1)} %copy-done.8, bf16[128,512]{1,0:T(8,128)(2,1)} %copy-done.11, bf16[128,512]{1,0:T(8,128)(2,1)} %copy-done.10, ...), custom_call_target="tpu_custom_call" | custom-call | tf_op jit(solution)/shard_map/send_part/pallas_call | solution.py:68
  158.8 4.0 %collective-permute-start.15 = (bf16[448,512]{1,0:T(8,128)(2,1)}, bf16[448,512]{1,0:T(8,128)(2,1)}, u32[]{:S(2)}, u32[]{:S(2)}) collective-permute-start(bf16[448,512]{1,0:T(8,128)(2,1)} %send_part.3), channel_id=1, source_target_pairs={{0,1},{1,0},{2,3},{3,2},{4,5},{5,4},{6,7},{7,6},{8,9},{9,8},{10,11... | collective-permute-start | bytes 1376264 | tf_op jit(solution)/shard_map/ppermute | solution.py:21
  162.8 1.8 collective-permute-done.15.refs_8_
  164.6 3.6 %step.3 = (bf16[448,2048]{1,0:T(8,128)(2,1)}, bf16[224,128]{1,0:T(8,128)(2,1)}, bf16[224,128]{1,0:T(8,128)(2,1)}, bf16[224,128]{1,0:T(8,128)(2,1)}, bf16[224,128...) custom-call(bf16[8,896,128]{2,1,0:T(8,128)(2,1)} %all-to-all-done.ac, ...), custom_call_target="tpu_custom_call", output_to_operand_aliasing={{0}: (12, {})} | custom-call | tf_op jit(solution)/shard_map/step/pallas_call | solution.py:128
  168.2 0.9 collective-permute-start.16
  169.2 4.4 %collective-permute-start.17 = (bf16[224,128]{1,0:T(8,128)(2,1)}, bf16[224,128]{1,0:T(8,128)(2,1)S(1)}, u32[]{:S(2)}, u32[]{:S(2)}) collective-permute-start(bf16[224,128]{1,0:T(8,128)(2,1)} %get-tuple-element.25), channel_id=1, source_target_pairs={{0,32},{16,48},{32,64},{48,80},{64,96},{80,112},{96,0},{112,16},{1... | collective-permute-start | bytes 172040 | tf_op jit(solution)/shard_map/ppermute | solution.py:294
  173.6 1.3 collective-permute-start.18
  174.8 4.3 %collective-permute-start.19 = (bf16[224,128]{1,0:T(8,128)(2,1)}, bf16[224,128]{1,0:T(8,128)(2,1)S(1)}, u32[]{:S(2)}, u32[]{:S(2)}) collective-permute-start(bf16[224,128]{1,0:T(8,128)(2,1)} %get-tuple-element.27), channel_id=1, source_target_pairs={{0,64},{16,80},{32,96},{48,112},{64,0},{80,16},{96,32},{112,48},{1... | collective-permute-start | bytes 172040 | tf_op jit(solution)/shard_map/ppermute | solution.py:294
  179.1 0.2 collective-permute-start.20
  179.3 3.4 %collective-permute-start.21 = (bf16[224,128]{1,0:T(8,128)(2,1)}, bf16[224,128]{1,0:T(8,128)(2,1)S(1)}, u32[]{:S(2)}, u32[]{:S(2)}) collective-permute-start(bf16[224,128]{1,0:T(8,128)(2,1)} %get-tuple-element.29), channel_id=1, source_target_pairs={{0,96},{16,112},{32,0},{48,16},{64,32},{80,48},{96,64},{112,80},{1... | collective-permute-start | bytes 172040 | tf_op jit(solution)/shard_map/ppermute | solution.py:294
  182.7 1.4 collective-permute-start.22
  184.1 1.4 collective-permute-start.23
  185.5 1.2 collective-permute-start.24
  186.7 0.7 collective-permute-start.25
  187.3 2.4 %collective-permute-done.21.refs_6_ = bf16[224,128]{1,0:T(8,128)(2,1)S(1)} collective-permute-done((bf16[224,128]{1,0:T(8,128)(2,1)}, bf16[224,128]{1,0:T(8,128)(2,1)S(1)}, u32[]{:S(2)}, u32[]{:S(2)}) %collective-permute-start.21) | collective-permute-done | bytes 57376 | tf_op jit(solution)/shard_map/ppermute | solution.py:294
  189.7 1.7 collective-permute-start.26
  191.6 1.4 collective-permute-start.28
  193.1 1.4 collective-permute-start.30
  194.4 0.3 collective-permute-done.27.refs_12_
  194.7 1.0 collective-permute-done.28.refs_13_
  195.7 1.2 collective-permute-done.29.refs_14_
  196.9 1.2 collective-permute-done.30.refs_15_
  198.3 0.6 copy-done.27
  198.9 2.6 %trim_apart.1 = (bf16[224,128]{1,0:T(8,128)(2,1)}, bf16[224,128]{1,0:T(8,128)(2,1)}, bf16[224,128]{1,0:T(8,128)(2,1)}, bf16[224,128]{1,0:T(8,128)(2,1)}, bf16[22...) custom-call(bf16[224,128]{1,0:T(8,128)(2,1)} %get-tuple-element.23.refs_0_, ...), custom_call_target="tpu_custom_call" | custom-call | tf_op jit(solution)/shard_map/trim_apart/pallas_call | solution.py:224
  201.5 1.4 collective-permute-start.31
  202.9 3.4 %collective-permute-start.33 = (bf16[224,128]{1,0:T(8,128)(2,1)}, bf16[224,128]{1,0:T(8,128)(2,1)}, u32[]{:S(2)}, u32[]{:S(2)}) collective-permute-start(bf16[224,128]{1,0:T(8,128)(2,1)} %get-tuple-element.34), channel_id=1, source_target_pairs={{0,48},{16,64},{32,80},{48,96},{64,112},{80,0},{96,16},{112,32},{1... | collective-permute-start | bytes 172040 | tf_op jit(solution)/shard_map/ppermute | solution.py:294
  206.2 2.1 collective-permute-start.34
  208.3 3.2 %collective-permute-start.35 = (bf16[224,128]{1,0:T(8,128)(2,1)}, bf16[224,128]{1,0:T(8,128)(2,1)}, u32[]{:S(2)}, u32[]{:S(2)}) collective-permute-start(bf16[224,128]{1,0:T(8,128)(2,1)} %get-tuple-element.36), channel_id=1, source_target_pairs={{0,80},{16,96},{32,112},{48,0},{64,16},{80,32},{96,48},{112,64},{1... | collective-permute-start | bytes 172040 | tf_op jit(solution)/shard_map/ppermute | solution.py:294
  211.5 2.1 collective-permute-start.36
  213.6 2.5 %lay.1.laid = bf16[448,2048]{1,0:T(8,128)(2,1)} custom-call(bf16[12,448,128]{2,1,0:T(8,128)(2,1)} %bitcast.7.piece), custom_call_target="tpu_custom_call" | custom-call | tf_op jit(solution)/shard_map/lay/pallas_call | solution.py:251
  216.2 3.4 %collective-permute-done.36.refs_6_ = bf16[224,128]{1,0:T(8,128)(2,1)} collective-permute-done((bf16[224,128]{1,0:T(8,128)(2,1)}, bf16[224,128]{1,0:T(8,128)(2,1)}, u32[]{:S(2)}, u32[]{:S(2)}) %collective-permute-start.36) | collective-permute-done | bytes 57376 | tf_op jit(solution)/shard_map/ppermute | solution.py:294
  219.6 0.8 collective-permute-done.37.refs_7_
  220.4 1.9 lay_apart.1
  (84 shorter events, 1.1 us)
Async XLA Ops:
  4.5 7.6 %copy-start = (bf16[1,128,2048]{2,1,0:T(8,128)(2,1)S(1)}, bf16[1,128,2048]{2,1,0:T(8,128)(2,1)}, u32[]{:S(2)}) copy-start(bf16[1,128,2048]{2,1,0:T(8,128)(2,1)} %param.5) | copy-start | bytes 1572868
  4.5 64.6 %all-to-all-start = ((bf16[8,896,128]{2,1,0:T(8,128)(2,1)}), bf16[8,896,128]{2,1,0:T(8,128)(2,1)}, u32[]{:S(2)}, u32[]{:S(2)}) async-start(bf16[8,896,128]{2,1,0:T(8,128)(2,1)} %bitcast.2), calls=%async_computation | async-start | bytes 3670016 | tf_op jit(solution)/shard_map/all_to_all | solution.py:307
  12.1 31.1 %collective-permute-start = (bf16[128,1536]{1,0:T(8,128)(2,1)S(1)}, bf16[128,1536]{1,0:T(8,128)(2,1)S(1)}, u32[]{:S(2)}, u32[]{:S(2)}) collective-permute-start(bf16[128,1536]{1,0:T(8,128)(2,1)S(1)} %slice.8), channel_id=1, source_target_pairs={{0,8},{1,9},{2,10},{3,11},{4,12},{5,13},{6,14},{7,15},{8,0},{9,1},... | collective-permute-start | bytes 1179656 | tf_op jit(solution)/shard_map/ppermute | solution.py:21
  15.2 31.9 %collective-permute-start.1 = (bf16[128,1536]{1,0:T(8,128)(2,1)S(1)}, bf16[128,1536]{1,0:T(8,128)(2,1)S(1)}, u32[]{:S(2)}, u32[]{:S(2)}) collective-permute-start(bf16[128,1536]{1,0:T(8,128)(2,1)S(1)} %slice.8), channel_id=1, source_target_pairs={{0,2},{1,3},{2,4},{3,5},{4,6},{5,7},{6,0},{7,1},{8,10},{9,11},{10,... | collective-permute-start | bytes 1179656 | tf_op jit(solution)/shard_map/ppermute | solution.py:21
  43.2 3.0 %copy-start.1 = (bf16[128,1536]{1,0:T(8,128)(2,1)}, bf16[128,1536]{1,0:T(8,128)(2,1)S(1)}, u32[]{:S(2)}) copy-start(bf16[128,1536]{1,0:T(8,128)(2,1)S(1)} %collective-permute-done.refs_1_) | copy-start | bytes 1179652
  43.2 9.0 %collective-permute-start.4 = (bf16[128,1536]{1,0:T(8,128)(2,1)S(1)}, bf16[128,1536]{1,0:T(8,128)(2,1)S(1)}, u32[]{:S(2)}, u32[]{:S(2)}) collective-permute-start(bf16[128,1536]{1,0:T(8,128)(2,1)S(1)} %collective-permute-done.refs_1_), channel_id=1, source_target_pairs={{0,6},{1,7},{2,0},{3,1},{4,2},{5,3},{6,4},{7,5},{8,14},{9,15},{10,... | collective-permute-start | bytes 1179656 | tf_op jit(solution)/shard_map/ppermute | solution.py:21
  45.7 15.0 %collective-permute-start.3 = (bf16[128,1536]{1,0:T(8,128)(2,1)S(1)}, bf16[128,1536]{1,0:T(8,128)(2,1)S(1)}, u32[]{:S(2)}, u32[]{:S(2)}) collective-permute-start(bf16[128,1536]{1,0:T(8,128)(2,1)S(1)} %slice.8), channel_id=1, source_target_pairs={{0,6},{1,7},{2,0},{3,1},{4,2},{5,3},{6,4},{7,5},{8,14},{9,15},{10,... | collective-permute-start | bytes 1179656 | tf_op jit(solution)/shard_map/ppermute | solution.py:21
  46.2 14.5 %collective-permute-start.2 = (bf16[128,1536]{1,0:T(8,128)(2,1)S(1)}, bf16[128,1536]{1,0:T(8,128)(2,1)S(1)}, u32[]{:S(2)}, u32[]{:S(2)}) collective-permute-start(bf16[128,1536]{1,0:T(8,128)(2,1)S(1)} %collective-permute-done.refs_1_), channel_id=1, source_target_pairs={{0,2},{1,3},{2,4},{3,5},{4,6},{5,7},{6,0},{7,1},{8,10},{9,11},{10,... | collective-permute-start | bytes 1179656 | tf_op jit(solution)/shard_map/ppermute | solution.py:21
  47.1 13.6 %copy-start.2 = (bf16[128,1536]{1,0:T(8,128)(2,1)}, bf16[128,1536]{1,0:T(8,128)(2,1)S(1)}, u32[]{:S(2)}) copy-start(bf16[128,1536]{1,0:T(8,128)(2,1)S(1)} %collective-permute-done.1.refs_2_) | copy-start | bytes 1179652
  47.1 16.9 %collective-permute-start.5 = (bf16[128,1536]{1,0:T(8,128)(2,1)S(1)}, bf16[128,1536]{1,0:T(8,128)(2,1)S(1)}, u32[]{:S(2)}, u32[]{:S(2)}) collective-permute-start(bf16[128,1536]{1,0:T(8,128)(2,1)S(1)} %collective-permute-done.1.refs_2_), channel_id=1, source_target_pairs={{0,2},{1,3},{2,4},{3,5},{4,6},{5,7},{6,0},{7,1},{8,10},{9,11},{10,... | collective-permute-start | bytes 1179656 | tf_op jit(solution)/shard_map/ppermute | solution.py:21
  52.3 11.8 %copy-start.3 = (bf16[128,1536]{1,0:T(8,128)(2,1)}, bf16[128,1536]{1,0:T(8,128)(2,1)S(1)}, u32[]{:S(2)}) copy-start(bf16[128,1536]{1,0:T(8,128)(2,1)S(1)} %collective-permute-done.4.refs_5_) | copy-start | bytes 1179652
  52.3 16.9 %collective-permute-start.6 = (bf16[128,1536]{1,0:T(8,128)(2,1)S(1)}, bf16[128,1536]{1,0:T(8,128)(2,1)}, u32[]{:S(2)}, u32[]{:S(2)}) collective-permute-start(bf16[128,1536]{1,0:T(8,128)(2,1)S(1)} %collective-permute-done.4.refs_5_), channel_id=1, source_target_pairs={{0,6},{1,7},{2,0},{3,1},{4,2},{5,3},{6,4},{7,5},{8,14},{9,15},{10,... | collective-permute-start | bytes 1179656 | tf_op jit(solution)/shard_map/ppermute | solution.py:21
  60.7 3.4 %copy-start.4 = (bf16[128,1536]{1,0:T(8,128)(2,1)}, bf16[128,1536]{1,0:T(8,128)(2,1)S(1)}, u32[]{:S(2)}) copy-start(bf16[128,1536]{1,0:T(8,128)(2,1)S(1)} %collective-permute-done.3.refs_4_) | copy-start | bytes 1179652
  60.7 3.4 %copy-start.5 = (bf16[128,1536]{1,0:T(8,128)(2,1)}, bf16[128,1536]{1,0:T(8,128)(2,1)S(1)}, u32[]{:S(2)}) copy-start(bf16[128,1536]{1,0:T(8,128)(2,1)S(1)} %collective-permute-done.2.refs_3_) | copy-start | bytes 1179652
  73.6 5.8 %collective-permute-start.7 = (bf16[448,1536]{1,0:T(8,128)(2,1)}, bf16[448,1536]{1,0:T(8,128)(2,1)}, u32[]{:S(2)}, u32[]{:S(2)}) collective-permute-start(bf16[448,1536]{1,0:T(8,128)(2,1)} %send_part.2), channel_id=1, source_target_pairs={{0,1},{1,0},{2,3},{3,2},{4,5},{5,4},{6,7},{7,6},{8,9},{9,8},{10,11... | collective-permute-start | bytes 4128776 | tf_op jit(solution)/shard_map/ppermute | solution.py:21
  130.1 83.5 %all-to-all-start.2 = ((bf16[16,336,128]{2,1,0:T(8,128)(2,1)}), bf16[16,336,128]{2,1,0:T(8,128)(2,1)}, u32[]{:S(2)}, u32[]{:S(2)}) async-start(bf16[16,336,128]{2,1,0:T(8,128)(2,1)} %trim.1), calls=%async_computation.2 | async-start | bytes 2752512 | tf_op jit(solution)/shard_map/all_to_all | solution.py:299
  136.7 7.8 %collective-permute-start.8 = (bf16[128,512]{1,0:T(8,128)(2,1)S(1)}, bf16[128,512]{1,0:T(8,128)(2,1)S(1)}, u32[]{:S(2)}, u32[]{:S(2)}) collective-permute-start(bf16[128,512]{1,0:T(8,128)(2,1)S(1)} %slice.9), channel_id=1, source_target_pairs={{0,8},{1,9},{2,10},{3,11},{4,12},{5,13},{6,14},{7,15},{8,0},{9,1},... | collective-permute-start | bytes 393224 | tf_op jit(solution)/shard_map/ppermute | solution.py:21
  137.4 12.0 %collective-permute-start.9 = (bf16[128,512]{1,0:T(8,128)(2,1)S(1)}, bf16[128,512]{1,0:T(8,128)(2,1)S(1)}, u32[]{:S(2)}, u32[]{:S(2)}) collective-permute-start(bf16[128,512]{1,0:T(8,128)(2,1)S(1)} %slice.9), channel_id=1, source_target_pairs={{0,2},{1,3},{2,4},{3,5},{4,6},{5,7},{6,0},{7,1},{8,10},{9,11},{10,... | collective-permute-start | bytes 393224 | tf_op jit(solution)/shard_map/ppermute | solution.py:21
  144.5 3.5 %copy-start.7 = (bf16[128,512]{1,0:T(8,128)(2,1)}, bf16[128,512]{1,0:T(8,128)(2,1)S(1)}, u32[]{:S(2)}) copy-start(bf16[128,512]{1,0:T(8,128)(2,1)S(1)} %collective-permute-done.8.refs_1_) | copy-start | bytes 393220
  144.5 5.5 %collective-permute-start.12 = (bf16[128,512]{1,0:T(8,128)(2,1)S(1)}, bf16[128,512]{1,0:T(8,128)(2,1)S(1)}, u32[]{:S(2)}, u32[]{:S(2)}) collective-permute-start(bf16[128,512]{1,0:T(8,128)(2,1)S(1)} %collective-permute-done.8.refs_1_), channel_id=1, source_target_pairs={{0,6},{1,7},{2,0},{3,1},{4,2},{5,3},{6,4},{7,5},{8,14},{9,15},{10,... | collective-permute-start | bytes 393224 | tf_op jit(solution)/shard_map/ppermute | solution.py:21
  148.0 5.3 %collective-permute-start.11 = (bf16[128,512]{1,0:T(8,128)(2,1)S(1)}, bf16[128,512]{1,0:T(8,128)(2,1)S(1)}, u32[]{:S(2)}, u32[]{:S(2)}) collective-permute-start(bf16[128,512]{1,0:T(8,128)(2,1)S(1)} %slice.9), channel_id=1, source_target_pairs={{0,6},{1,7},{2,0},{3,1},{4,2},{5,3},{6,4},{7,5},{8,14},{9,15},{10,... | collective-permute-start | bytes 393224 | tf_op jit(solution)/shard_map/ppermute | solution.py:21
  148.0 5.4 %collective-permute-start.10 = (bf16[128,512]{1,0:T(8,128)(2,1)S(1)}, bf16[128,512]{1,0:T(8,128)(2,1)S(1)}, u32[]{:S(2)}, u32[]{:S(2)}) collective-permute-start(bf16[128,512]{1,0:T(8,128)(2,1)S(1)} %collective-permute-done.8.refs_1_), channel_id=1, source_target_pairs={{0,2},{1,3},{2,4},{3,5},{4,6},{5,7},{6,0},{7,1},{8,10},{9,11},{10,... | collective-permute-start | bytes 393224 | tf_op jit(solution)/shard_map/ppermute | solution.py:21
  149.5 4.0 %copy-start.8 = (bf16[128,512]{1,0:T(8,128)(2,1)}, bf16[128,512]{1,0:T(8,128)(2,1)S(1)}, u32[]{:S(2)}) copy-start(bf16[128,512]{1,0:T(8,128)(2,1)S(1)} %collective-permute-done.9.refs_2_) | copy-start | bytes 393220
  149.5 5.4 %collective-permute-start.13 = (bf16[128,512]{1,0:T(8,128)(2,1)S(1)}, bf16[128,512]{1,0:T(8,128)(2,1)S(1)}, u32[]{:S(2)}, u32[]{:S(2)}) collective-permute-start(bf16[128,512]{1,0:T(8,128)(2,1)S(1)} %collective-permute-done.9.refs_2_), channel_id=1, source_target_pairs={{0,2},{1,3},{2,4},{3,5},{4,6},{5,7},{6,0},{7,1},{8,10},{9,11},{10,... | collective-permute-start | bytes 393224 | tf_op jit(solution)/shard_map/ppermute | solution.py:21
  150.0 5.0 %copy-start.9 = (bf16[128,512]{1,0:T(8,128)(2,1)}, bf16[128,512]{1,0:T(8,128)(2,1)S(1)}, u32[]{:S(2)}) copy-start(bf16[128,512]{1,0:T(8,128)(2,1)S(1)} %collective-permute-done.12.refs_5_) | copy-start | bytes 393220
  150.0 5.8 %collective-permute-start.14 = (bf16[128,512]{1,0:T(8,128)(2,1)S(1)}, bf16[128,512]{1,0:T(8,128)(2,1)}, u32[]{:S(2)}, u32[]{:S(2)}) collective-permute-start(bf16[128,512]{1,0:T(8,128)(2,1)S(1)} %collective-permute-done.12.refs_5_), channel_id=1, source_target_pairs={{0,6},{1,7},{2,0},{3,1},{4,2},{5,3},{6,4},{7,5},{8,14},{9,15},{10,... | collective-permute-start | bytes 393224 | tf_op jit(solution)/shard_map/ppermute | solution.py:21
  153.3 1.6 copy-start.10
  153.5 1.5 copy-start.11
  158.8 5.8 %collective-permute-start.15 = (bf16[448,512]{1,0:T(8,128)(2,1)}, bf16[448,512]{1,0:T(8,128)(2,1)}, u32[]{:S(2)}, u32[]{:S(2)}) collective-permute-start(bf16[448,512]{1,0:T(8,128)(2,1)} %send_part.3), channel_id=1, source_target_pairs={{0,1},{1,0},{2,3},{3,2},{4,5},{5,4},{6,7},{7,6},{8,9},{9,8},{10,11... | collective-permute-start | bytes 1376264 | tf_op jit(solution)/shard_map/ppermute | solution.py:21
  168.2 11.0 %collective-permute-start.16 = (bf16[224,128]{1,0:T(8,128)(2,1)}, bf16[224,128]{1,0:T(8,128)(2,1)S(1)}, u32[]{:S(2)}, u32[]{:S(2)}) collective-permute-start(bf16[224,128]{1,0:T(8,128)(2,1)} %get-tuple-element.24), channel_id=1, source_target_pairs={{0,16},{16,32},{32,48},{48,64},{64,80},{80,96},{96,112},{112,0},{1... | collective-permute-start | bytes 172040 | tf_op jit(solution)/shard_map/ppermute | solution.py:294
  169.2 13.5 %collective-permute-start.17 = (bf16[224,128]{1,0:T(8,128)(2,1)}, bf16[224,128]{1,0:T(8,128)(2,1)S(1)}, u32[]{:S(2)}, u32[]{:S(2)}) collective-permute-start(bf16[224,128]{1,0:T(8,128)(2,1)} %get-tuple-element.25), channel_id=1, source_target_pairs={{0,32},{16,48},{32,64},{48,80},{64,96},{80,112},{96,0},{112,16},{1... | collective-permute-start | bytes 172040 | tf_op jit(solution)/shard_map/ppermute | solution.py:294
  173.6 10.5 %collective-permute-start.18 = (bf16[224,128]{1,0:T(8,128)(2,1)}, bf16[224,128]{1,0:T(8,128)(2,1)S(1)}, u32[]{:S(2)}, u32[]{:S(2)}) collective-permute-start(bf16[224,128]{1,0:T(8,128)(2,1)} %get-tuple-element.26), channel_id=1, source_target_pairs={{0,48},{16,64},{32,80},{48,96},{64,112},{80,0},{96,16},{112,32},{1... | collective-permute-start | bytes 172040 | tf_op jit(solution)/shard_map/ppermute | solution.py:294
  174.8 10.7 %collective-permute-start.19 = (bf16[224,128]{1,0:T(8,128)(2,1)}, bf16[224,128]{1,0:T(8,128)(2,1)S(1)}, u32[]{:S(2)}, u32[]{:S(2)}) collective-permute-start(bf16[224,128]{1,0:T(8,128)(2,1)} %get-tuple-element.27), channel_id=1, source_target_pairs={{0,64},{16,80},{32,96},{48,112},{64,0},{80,16},{96,32},{112,48},{1... | collective-permute-start | bytes 172040 | tf_op jit(solution)/shard_map/ppermute | solution.py:294
  179.1 7.6 %collective-permute-start.20 = (bf16[224,128]{1,0:T(8,128)(2,1)}, bf16[224,128]{1,0:T(8,128)(2,1)S(1)}, u32[]{:S(2)}, u32[]{:S(2)}) collective-permute-start(bf16[224,128]{1,0:T(8,128)(2,1)} %get-tuple-element.28), channel_id=1, source_target_pairs={{0,80},{16,96},{32,112},{48,0},{64,16},{80,32},{96,48},{112,64},{1... | collective-permute-start | bytes 172040 | tf_op jit(solution)/shard_map/ppermute | solution.py:294
  179.3 18.9 %copy-start.13 = (bf16[224,128]{1,0:T(8,128)(2,1)}, bf16[224,128]{1,0:T(8,128)(2,1)S(1)}, u32[]{:S(2)}) copy-start(bf16[224,128]{1,0:T(8,128)(2,1)S(1)} %collective-permute-done.16.refs_1_) | copy-start | bytes 172036
  179.3 10.4 %collective-permute-start.21 = (bf16[224,128]{1,0:T(8,128)(2,1)}, bf16[224,128]{1,0:T(8,128)(2,1)S(1)}, u32[]{:S(2)}, u32[]{:S(2)}) collective-permute-start(bf16[224,128]{1,0:T(8,128)(2,1)} %get-tuple-element.29), channel_id=1, source_target_pairs={{0,96},{16,112},{32,0},{48,16},{64,32},{80,48},{96,64},{112,80},{1... | collective-permute-start | bytes 172040 | tf_op jit(solution)/shard_map/ppermute | solution.py:294
  182.7 15.5 %copy-start.14 = (bf16[224,128]{1,0:T(8,128)(2,1)}, bf16[224,128]{1,0:T(8,128)(2,1)S(1)}, u32[]{:S(2)}) copy-start(bf16[224,128]{1,0:T(8,128)(2,1)S(1)} %collective-permute-done.17.refs_2_) | copy-start | bytes 172036
  182.7 8.8 %collective-permute-start.22 = (bf16[224,128]{1,0:T(8,128)(2,1)}, bf16[224,128]{1,0:T(8,128)(2,1)S(1)}, u32[]{:S(2)}, u32[]{:S(2)}) collective-permute-start(bf16[224,128]{1,0:T(8,128)(2,1)} %get-tuple-element.30), channel_id=1, source_target_pairs={{0,112},{16,0},{32,16},{48,32},{64,48},{80,64},{96,80},{112,96},{1... | collective-permute-start | bytes 172040 | tf_op jit(solution)/shard_map/ppermute | solution.py:294
  184.1 14.1 %copy-start.15 = (bf16[224,128]{1,0:T(8,128)(2,1)}, bf16[224,128]{1,0:T(8,128)(2,1)S(1)}, u32[]{:S(2)}) copy-start(bf16[224,128]{1,0:T(8,128)(2,1)S(1)} %collective-permute-done.18.refs_3_) | copy-start | bytes 172036
  184.1 7.5 %collective-permute-start.23 = (bf16[224,128]{1,0:T(8,128)(2,1)}, bf16[224,128]{1,0:T(8,128)(2,1)S(1)}, u32[]{:S(2)}, u32[]{:S(2)}) collective-permute-start(bf16[224,128]{1,0:T(8,128)(2,1)} %get-tuple-element.23.refs_0_), channel_id=1, source_target_pairs={{0,128},{16,144},{32,160},{48,176},{64,192},{80,208},{96,224},{112... | collective-permute-start | bytes 172040 | tf_op jit(solution)/shard_map/ppermute | solution.py:334
  185.5 12.7 %copy-start.16 = (bf16[224,128]{1,0:T(8,128)(2,1)}, bf16[224,128]{1,0:T(8,128)(2,1)S(1)}, u32[]{:S(2)}) copy-start(bf16[224,128]{1,0:T(8,128)(2,1)S(1)} %collective-permute-done.19.refs_4_) | copy-start | bytes 172036
  185.5 7.5 %collective-permute-start.24 = (bf16[224,128]{1,0:T(8,128)(2,1)S(1)}, bf16[224,128]{1,0:T(8,128)(2,1)S(1)}, u32[]{:S(2)}, u32[]{:S(2)}) collective-permute-start(bf16[224,128]{1,0:T(8,128)(2,1)S(1)} %collective-permute-done.16.refs_1_), channel_id=1, source_target_pairs={{0,128},{16,144},{32,160},{48,176},{64,192},{80,208},{96,224},{112... | collective-permute-start | bytes 172040 | tf_op jit(solution)/shard_map/ppermute | solution.py:334
  186.7 11.5 %copy-start.17 = (bf16[224,128]{1,0:T(8,128)(2,1)}, bf16[224,128]{1,0:T(8,128)(2,1)S(1)}, u32[]{:S(2)}) copy-start(bf16[224,128]{1,0:T(8,128)(2,1)S(1)} %collective-permute-done.20.refs_5_) | copy-start | bytes 172036
  186.7 6.4 %collective-permute-start.25 = (bf16[224,128]{1,0:T(8,128)(2,1)S(1)}, bf16[224,128]{1,0:T(8,128)(2,1)S(1)}, u32[]{:S(2)}, u32[]{:S(2)}) collective-permute-start(bf16[224,128]{1,0:T(8,128)(2,1)S(1)} %collective-permute-done.17.refs_2_), channel_id=1, source_target_pairs={{0,128},{16,144},{32,160},{48,176},{64,192},{80,208},{96,224},{112... | collective-permute-start | bytes 172040 | tf_op jit(solution)/shard_map/ppermute | solution.py:334
  189.7 8.4 %copy-start.18 = (bf16[224,128]{1,0:T(8,128)(2,1)}, bf16[224,128]{1,0:T(8,128)(2,1)S(1)}, u32[]{:S(2)}) copy-start(bf16[224,128]{1,0:T(8,128)(2,1)S(1)} %collective-permute-done.21.refs_6_) | copy-start | bytes 172036
  189.7 4.7 %collective-permute-start.26 = (bf16[224,128]{1,0:T(8,128)(2,1)S(1)}, bf16[224,128]{1,0:T(8,128)(2,1)S(1)}, u32[]{:S(2)}, u32[]{:S(2)}) collective-permute-start(bf16[224,128]{1,0:T(8,128)(2,1)S(1)} %collective-permute-done.18.refs_3_), channel_id=1, source_target_pairs={{0,128},{16,144},{32,160},{48,176},{64,192},{80,208},{96,224},{112... | collective-permute-start | bytes 172040 | tf_op jit(solution)/shard_map/ppermute | solution.py:334
  191.5 6.7 %copy-start.19 = (bf16[224,128]{1,0:T(8,128)(2,1)}, bf16[224,128]{1,0:T(8,128)(2,1)S(1)}, u32[]{:S(2)}) copy-start(bf16[224,128]{1,0:T(8,128)(2,1)S(1)} %collective-permute-done.22.refs_7_) | copy-start | bytes 172036
  191.5 3.2 %collective-permute-start.27 = (bf16[224,128]{1,0:T(8,128)(2,1)S(1)}, bf16[224,128]{1,0:T(8,128)(2,1)S(1)}, u32[]{:S(2)}, u32[]{:S(2)}) collective-permute-start(bf16[224,128]{1,0:T(8,128)(2,1)S(1)} %collective-permute-done.19.refs_4_), channel_id=1, source_target_pairs={{0,128},{16,144},{32,160},{48,176},{64,192},{80,208},{96,224},{112... | collective-permute-start | bytes 172040 | tf_op jit(solution)/shard_map/ppermute | solution.py:334
  191.6 6.6 %copy-start.20 = (bf16[224,128]{1,0:T(8,128)(2,1)}, bf16[224,128]{1,0:T(8,128)(2,1)S(1)}, u32[]{:S(2)}) copy-start(bf16[224,128]{1,0:T(8,128)(2,1)S(1)} %collective-permute-done.23.refs_8_) | copy-start | bytes 172036
  191.6 4.1 %collective-permute-start.28 = (bf16[224,128]{1,0:T(8,128)(2,1)S(1)}, bf16[224,128]{1,0:T(8,128)(2,1)S(1)}, u32[]{:S(2)}, u32[]{:S(2)}) collective-permute-start(bf16[224,128]{1,0:T(8,128)(2,1)S(1)} %collective-permute-done.20.refs_5_), channel_id=1, source_target_pairs={{0,128},{16,144},{32,160},{48,176},{64,192},{80,208},{96,224},{112... | collective-permute-start | bytes 172040 | tf_op jit(solution)/shard_map/ppermute | solution.py:334
  192.9 5.2 %copy-start.21 = (bf16[224,128]{1,0:T(8,128)(2,1)}, bf16[224,128]{1,0:T(8,128)(2,1)S(1)}, u32[]{:S(2)}) copy-start(bf16[224,128]{1,0:T(8,128)(2,1)S(1)} %collective-permute-done.24.refs_9_) | copy-start | bytes 172036
  193.0 4.0 %collective-permute-start.29 = (bf16[224,128]{1,0:T(8,128)(2,1)S(1)}, bf16[224,128]{1,0:T(8,128)(2,1)S(1)}, u32[]{:S(2)}, u32[]{:S(2)}) collective-permute-start(bf16[224,128]{1,0:T(8,128)(2,1)S(1)} %collective-permute-done.21.refs_6_), channel_id=1, source_target_pairs={{0,128},{16,144},{32,160},{48,176},{64,192},{80,208},{96,224},{112... | collective-permute-start | bytes 172040 | tf_op jit(solution)/shard_map/ppermute | solution.py:334
  193.1 5.1 %copy-start.22 = (bf16[224,128]{1,0:T(8,128)(2,1)}, bf16[224,128]{1,0:T(8,128)(2,1)S(1)}, u32[]{:S(2)}) copy-start(bf16[224,128]{1,0:T(8,128)(2,1)S(1)} %collective-permute-done.25.refs_10_) | copy-start | bytes 172036
  193.1 5.1 %collective-permute-start.30 = (bf16[224,128]{1,0:T(8,128)(2,1)S(1)}, bf16[224,128]{1,0:T(8,128)(2,1)S(1)}, u32[]{:S(2)}, u32[]{:S(2)}) collective-permute-start(bf16[224,128]{1,0:T(8,128)(2,1)S(1)} %collective-permute-done.22.refs_7_), channel_id=1, source_target_pairs={{0,128},{16,144},{32,160},{48,176},{64,192},{80,208},{96,224},{112... | collective-permute-start | bytes 172040 | tf_op jit(solution)/shard_map/ppermute | solution.py:334
  194.4 3.8 %copy-start.23 = (bf16[224,128]{1,0:T(8,128)(2,1)}, bf16[224,128]{1,0:T(8,128)(2,1)S(1)}, u32[]{:S(2)}) copy-start(bf16[224,128]{1,0:T(8,128)(2,1)S(1)} %collective-permute-done.26.refs_11_) | copy-start | bytes 172036
  194.7 3.5 %copy-start.24 = (bf16[224,128]{1,0:T(8,128)(2,1)}, bf16[224,128]{1,0:T(8,128)(2,1)S(1)}, u32[]{:S(2)}) copy-start(bf16[224,128]{1,0:T(8,128)(2,1)S(1)} %collective-permute-done.27.refs_12_) | copy-start | bytes 172036
  195.7 2.6 %copy-start.25 = (bf16[224,128]{1,0:T(8,128)(2,1)}, bf16[224,128]{1,0:T(8,128)(2,1)S(1)}, u32[]{:S(2)}) copy-start(bf16[224,128]{1,0:T(8,128)(2,1)S(1)} %collective-permute-done.28.refs_13_) | copy-start | bytes 172036
  201.5 10.0 %collective-permute-start.31 = (bf16[224,128]{1,0:T(8,128)(2,1)}, bf16[224,128]{1,0:T(8,128)(2,1)}, u32[]{:S(2)}, u32[]{:S(2)}) collective-permute-start(bf16[224,128]{1,0:T(8,128)(2,1)} %get-tuple-element.32), channel_id=1, source_target_pairs={{0,16},{16,32},{32,48},{48,64},{64,80},{80,96},{96,112},{112,0},{1... | collective-permute-start | bytes 172040 | tf_op jit(solution)/shard_map/ppermute | solution.py:294
  202.9 10.8 %collective-permute-start.32 = (bf16[224,128]{1,0:T(8,128)(2,1)}, bf16[224,128]{1,0:T(8,128)(2,1)}, u32[]{:S(2)}, u32[]{:S(2)}) collective-permute-start(bf16[224,128]{1,0:T(8,128)(2,1)} %get-tuple-element.33), channel_id=1, source_target_pairs={{0,32},{16,48},{32,64},{48,80},{64,96},{80,112},{96,0},{112,16},{1... | collective-permute-start | bytes 172040 | tf_op jit(solution)/shard_map/ppermute | solution.py:294
  202.9 13.3 %collective-permute-start.33 = (bf16[224,128]{1,0:T(8,128)(2,1)}, bf16[224,128]{1,0:T(8,128)(2,1)}, u32[]{:S(2)}, u32[]{:S(2)}) collective-permute-start(bf16[224,128]{1,0:T(8,128)(2,1)} %get-tuple-element.34), channel_id=1, source_target_pairs={{0,48},{16,64},{32,80},{48,96},{64,112},{80,0},{96,16},{112,32},{1... | collective-permute-start | bytes 172040 | tf_op jit(solution)/shard_map/ppermute | solution.py:294
  206.2 9.9 %collective-permute-start.34 = (bf16[224,128]{1,0:T(8,128)(2,1)}, bf16[224,128]{1,0:T(8,128)(2,1)}, u32[]{:S(2)}, u32[]{:S(2)}) collective-permute-start(bf16[224,128]{1,0:T(8,128)(2,1)} %get-tuple-element.35), channel_id=1, source_target_pairs={{0,64},{16,80},{32,96},{48,112},{64,0},{80,16},{96,32},{112,48},{1... | collective-permute-start | bytes 172040 | tf_op jit(solution)/shard_map/ppermute | solution.py:294
  208.3 7.8 %collective-permute-start.35 = (bf16[224,128]{1,0:T(8,128)(2,1)}, bf16[224,128]{1,0:T(8,128)(2,1)}, u32[]{:S(2)}, u32[]{:S(2)}) collective-permute-start(bf16[224,128]{1,0:T(8,128)(2,1)} %get-tuple-element.36), channel_id=1, source_target_pairs={{0,80},{16,96},{32,112},{48,0},{64,16},{80,32},{96,48},{112,64},{1... | collective-permute-start | bytes 172040 | tf_op jit(solution)/shard_map/ppermute | solution.py:294
  211.5 8.1 %collective-permute-start.36 = (bf16[224,128]{1,0:T(8,128)(2,1)}, bf16[224,128]{1,0:T(8,128)(2,1)}, u32[]{:S(2)}, u32[]{:S(2)}) collective-permute-start(bf16[224,128]{1,0:T(8,128)(2,1)} %get-tuple-element.37), channel_id=1, source_target_pairs={{0,96},{16,112},{32,0},{48,16},{64,32},{80,48},{96,64},{112,80},{1... | collective-permute-start | bytes 172040 | tf_op jit(solution)/shard_map/ppermute | solution.py:294
  213.6 6.8 %collective-permute-start.37 = (bf16[224,128]{1,0:T(8,128)(2,1)}, bf16[224,128]{1,0:T(8,128)(2,1)}, u32[]{:S(2)}, u32[]{:S(2)}) collective-permute-start(bf16[224,128]{1,0:T(8,128)(2,1)} %get-tuple-element.38), channel_id=1, source_target_pairs={{0,112},{16,0},{32,16},{48,32},{64,48},{80,64},{96,80},{112,96},{1... | collective-permute-start | bytes 172040 | tf_op jit(solution)/shard_map/ppermute | solution.py:294
  (4 other events, 3.4 us)
